TPU v7x, 256 devices: a whole 4x4x8 slice. The times are simulated.
256 devices in a mesh: dp: 4 (over y), expert: 64 (over z, x, core).
Axes of the slice: x: 4, y: 4, z: 8, core: 2. Of those that a mesh axis runs over, the one named last changes fastest.
Arguments:
- tokens: bfloat16 [16384, 2048], P(('dp', 'expert')), may hold values from -6 to 6
- expert_ids: int32 [16384, 6], P(('dp', 'expert')), may hold values from 0 to 63, as said below
- gate_probs: float32 [16384, 6], P(('dp', 'expert')), may hold values from 0.1 to 0.5
- cotangent: bfloat16 [16384, 2048], P(('dp', 'expert')), may hold values from -6 to 6
- gate_proj: bfloat16 [64, 2048, 768], P('expert', 'dp'), may hold values from -0.125 to 0.125
- up_proj: bfloat16 [64, 2048, 768], P('expert', 'dp'), may hold values from -0.125 to 0.125
- down_proj: bfloat16 [64, 2048, 768], P('expert', 'dp'), may hold values from -0.21875 to 0.21875
Outputs:
- mixed: bfloat16 [16384, 2048], P(('dp', 'expert'))
- token_grads: bfloat16 [16384, 2048], P(('dp', 'expert'))
- prob_grads: float32 [16384, 6], P(('dp', 'expert'))
- grad_gate_proj: float32 [64, 2048, 768], P('expert', 'dp')
- grad_up_proj: float32 [64, 2048, 768], P('expert', 'dp')
- grad_down_proj: float32 [64, 2048, 768], P('expert', 'dp')
Inputs may be any that keep to these rules, and one draw needn't show every extreme that they name: `expert_ids`: each row names 6 different experts. Among the 64 rows of one device no expert is named by more than 8 rows, and in every data group some expert is named by exactly 8 rows of every device of that group.
All inputs are finite; a program needn't handle non-finite values.
Results may differ from a plain program's by a relative error of at most 0.0065.
Values may be sent and summed in bfloat16 or wider, within the bound.
A program may use at most 128 MiB of HBM per device.

v0:
```python
import jax
import jax.numpy as jnp
from jax import lax
from jax.sharding import PartitionSpec as P


def routing_slots(expert_ids, experts):
    onehot = (expert_ids[:, :, None] == jnp.arange(experts, dtype=jnp.int32)[None, None, :]).astype(
        jnp.int32
    )
    per_token = jnp.sum(onehot, axis=1)
    earlier = jnp.cumsum(per_token, axis=0) - per_token
    return jnp.sum(onehot * earlier[:, None, :], axis=2)


def forward_rows(rows, gate_proj, up_proj, down_proj):
    gate_pre = jnp.dot(rows, gate_proj, preferred_element_type=jnp.float32)
    up_pre = jnp.dot(rows, up_proj, preferred_element_type=jnp.float32)
    hidden = (jax.nn.silu(gate_pre) * up_pre).astype(jnp.bfloat16)
    expert_out = lax.dot_general(
        hidden, down_proj, (((1,), (1,)), ((), ())), preferred_element_type=jnp.float32
    ).astype(jnp.bfloat16)
    return (expert_out, gate_pre, up_pre, hidden)


def backward_rows(grad_rows, gate_pre, up_pre, gate_proj, up_proj, down_proj):
    d_hidden = jnp.dot(grad_rows, down_proj, preferred_element_type=jnp.float32)
    sigmoid_gate = jax.nn.sigmoid(gate_pre)
    silu_gate = gate_pre * sigmoid_gate
    d_gate = (d_hidden * up_pre * sigmoid_gate * (1.0 + gate_pre * (1.0 - sigmoid_gate))).astype(
        jnp.bfloat16
    )
    d_up = (d_hidden * silu_gate).astype(jnp.bfloat16)
    across = (((1,), (1,)), ((), ()))
    d_rows = lax.dot_general(d_gate, gate_proj, across, preferred_element_type=jnp.float32)
    d_rows = d_rows + lax.dot_general(d_up, up_proj, across, preferred_element_type=jnp.float32)
    return (d_rows.astype(jnp.bfloat16), d_gate, d_up)


def pick_rows(source_rows, position, top_count):
    chosen = jnp.take(source_rows, position.reshape(-1), axis=0)
    return chosen.reshape(position.shape[0], top_count, source_rows.shape[1])


def on_device(tokens, expert_ids, gate_probs, cotangent, gate_proj, up_proj, down_proj):
    experts = lax.axis_size("expert")
    tok_dev, top_count = expert_ids.shape
    model_width = tokens.shape[1]
    capacity = min(tok_dev, (tok_dev * top_count * 4 + 3 * experts - 1) // (3 * experts))
    slot_index = routing_slots(expert_ids, experts)
    position = expert_ids * capacity + slot_index
    placing = (
        position[None, :, :] == jnp.arange(experts * capacity, dtype=jnp.int32)[:, None, None]
    ).astype(jnp.float32)
    placer = jnp.sum(placing, axis=2)
    weighted = jnp.sum(placing * gate_probs[None, :, :], axis=2)
    row_send = (
        jnp.dot(placer.astype(jnp.bfloat16), tokens, preferred_element_type=jnp.float32)
        .astype(jnp.bfloat16)
        .reshape(experts, capacity, model_width)
    )
    grad_send = (
        jnp.dot(weighted, cotangent.astype(jnp.float32), precision=lax.Precision.HIGHEST)
        .astype(jnp.bfloat16)
        .reshape(experts, capacity, model_width)
    )
    full_gate, full_up, full_down = (
        lax.all_gather(gate_proj[0], "dp", axis=0, tiled=True),
        lax.all_gather(up_proj[0], "dp", axis=0, tiled=True),
        lax.all_gather(down_proj[0], "dp", axis=0, tiled=True),
    )
    rows_in = lax.all_to_all(row_send, "expert", split_axis=0, concat_axis=0, tiled=True)
    rows_flat = rows_in.reshape(-1, model_width)
    expert_out, gate_pre, up_pre, hidden = forward_rows(rows_flat, full_gate, full_up, full_down)
    returned = lax.all_to_all(
        expert_out.reshape(experts, capacity, model_width),
        "expert",
        split_axis=0,
        concat_axis=0,
        tiled=True,
    )
    grads_in = lax.all_to_all(grad_send, "expert", split_axis=0, concat_axis=0, tiled=True)
    grads_flat = grads_in.reshape(-1, model_width)
    d_rows, d_gate, d_up = backward_rows(
        grads_flat, gate_pre, up_pre, full_gate, full_up, full_down
    )
    grad_back = lax.all_to_all(
        d_rows.reshape(experts, capacity, model_width),
        "expert",
        split_axis=0,
        concat_axis=0,
        tiled=True,
    )
    picked = pick_rows(returned.reshape(-1, model_width), position, top_count).astype(jnp.float32)
    mixed = jnp.sum(gate_probs[:, :, None] * picked, axis=1).astype(jnp.bfloat16)
    prob_grads = jnp.sum(cotangent.astype(jnp.float32)[:, None, :] * picked, axis=2)
    picked_grads = pick_rows(grad_back.reshape(-1, model_width), position, top_count).astype(
        jnp.float32
    )
    token_grads = jnp.sum(picked_grads, axis=1).astype(jnp.bfloat16)
    contract_rows = (((0,), (0,)), ((), ()))
    hidden_units = hidden.shape[1]
    gate_term = lax.dot_general(
        rows_flat, d_gate, contract_rows, preferred_element_type=jnp.float32
    )
    up_term = lax.dot_general(rows_flat, d_up, contract_rows, preferred_element_type=jnp.float32)
    down_term = lax.dot_general(
        grads_flat, hidden, contract_rows, preferred_element_type=jnp.float32
    )
    shares = lax.psum_scatter(
        jnp.concatenate([gate_term, up_term, down_term], axis=1),
        "dp",
        scatter_dimension=0,
        tiled=True,
    )
    grad_gate = shares[:, :hidden_units]
    grad_up = shares[:, hidden_units : 2 * hidden_units]
    grad_down = shares[:, 2 * hidden_units :]
    return (mixed, token_grads, prob_grads, grad_gate[None], grad_up[None], grad_down[None])


def solution(mesh):
    in_specs = (
        P(("dp", "expert"), None),
        P(("dp", "expert"), None),
        P(("dp", "expert"), None),
        P(("dp", "expert"), None),
        P("expert", "dp", None),
        P("expert", "dp", None),
        P("expert", "dp", None),
    )
    out_specs = (
        P(("dp", "expert"), None),
        P(("dp", "expert"), None),
        P(("dp", "expert"), None),
        P("expert", "dp", None),
        P("expert", "dp", None),
        P("expert", "dp", None),
    )
    return jax.shard_map(
        on_device, mesh=mesh, in_specs=in_specs, out_specs=out_specs, check_vma=False
    )
```

profile of v0, /device:TPU:2, one launch (start us, length us, event | category | flops | bytes accessed | tf_op | source)
XLA Modules:
  0.0 345.9 jit_solution(1799393271010619139)
XLA Ops:
  7.2 0.0 copy-start
  7.2 0.0 copy-start.5
  7.2 0.0 all-gather.11.cloned.1.call-start
  7.2 0.7 all-gather.11.cloned.1.call-update
  7.9 0.0 all-gather.9.cloned.1.call-start
  8.0 0.7 all-gather.9.cloned.1.call-update
  8.7 0.8 convert_reduce_fusion.1
  9.5 0.1 reduce_window_sum.11
  9.6 1.0 select_reduce_fusion.1
  10.6 0.7 multiply_add_fusion
  11.2 0.9 select_reduce_fusion
  12.2 0.0 copy-done.5
  12.2 3.2 fusion.18
  15.4 12.0 %all-to-all-start.2 = ((bf16[64,8,2048]{2,1,0:T(8,128)(2,1)}), bf16[64,8,2048]{2,1,0:T(8,128)(2,1)S(1)}, u32[]{:S(2)}, u32[]{:S(2)}) async-start(bf16[64,8,2048]{2,1,0:T(8,128)(2,1)} %fusion.18), calls=%async_computation.2 | async-start | bytes 4194304 | tf_op jit(solution)/shard_map/all_to_all | solution.py:82
  27.4 0.0 all-gather.7.cloned.1.call-start
  27.4 0.7 all-gather.7.cloned.1.call-update
  28.1 0.0 copy-done
  28.1 2.0 fusion.17
  30.2 48.5 %all-to-all-done.2 = bf16[64,8,2048]{2,1,0:T(8,128)(2,1)S(1)} async-done(((bf16[64,8,2048]{2,1,0:T(8,128)(2,1)}), bf16[64,8,2048]{2,1,0:T(8,128)(2,1)S(1)}, u32[]{:S(2)}, u32[]{:S(2)}) %all-to-all-start.2) | async-done | bytes 2097184 | tf_op jit(solution)/shard_map/all_to_all | solution.py:82
  78.6 1.3 copy-done.3
  80.0 5.4 %all-to-all-start = ((bf16[64,8,2048]{2,1,0:T(8,128)(2,1)}), bf16[64,8,2048]{2,1,0:T(8,128)(2,1)S(1)}, u32[]{:S(2)}, u32[]{:S(2)}) async-start(bf16[64,8,2048]{2,1,0:T(8,128)(2,1)} %fusion.17), calls=%async_computation | async-start | bytes 4194304 | tf_op jit(solution)/shard_map/all_to_all | solution.py:72
  85.4 0.2 reduce-scatter.2.cloned.1.call-start
  85.7 0.0 all-gather.11.cloned.1.call-done
  85.7 5.5 %fusion = f32[512,768]{1,0:T(8,128)} fusion(bf16[1,2048,768]{2,1,0:T(8,128)(2,1)} %all-gather.11.cloned.1.call-done, bf16[64,8,2048]{2,1,0:T(8,128)(2,1)} %copy-done.3), kind=kOutput, calls=%fused_computation.5 | convolution fusion | flops 1610612736 | bytes 6815744 | tf_op jit(solution)/shard_map/dot_general | solution.py:27
  91.2 45.5 %all-to-all-done = bf16[64,8,2048]{2,1,0:T(8,128)(2,1)S(1)} async-done(((bf16[64,8,2048]{2,1,0:T(8,128)(2,1)}), bf16[64,8,2048]{2,1,0:T(8,128)(2,1)S(1)}, u32[]{:S(2)}, u32[]{:S(2)}) %all-to-all-start) | async-done | bytes 2097184 | tf_op jit(solution)/shard_map/all_to_all | solution.py:72
  136.7 4.8 %fusion.6 = f32[512,768]{1,0:T(8,128)} fusion(bf16[1,2048,768]{2,1,0:T(8,128)(2,1)} %all-gather.9.cloned.1.call-done, bf16[64,8,2048]{2,1,0:T(8,128)(2,1)S(1)} %all-to-all-done), kind=kOutput, calls=%fused_computation.11 | convolution fusion | flops 1610612736 | bytes 6815744 | tf_op jit(solution)/shard_map/dot_general | solution.py:18
  141.5 1.8 all-gather.7.cloned.1.call-done
  143.3 5.3 %multiply_convert_fusion.1 = (bf16[512,768]{1,0:T(8,128)(2,1)S(1)}, bf16[512,768]{1,0:T(8,128)(2,1)S(1)}, bf16[512,768]{1,0:T(8,128)(2,1)S(1)}) fusion(f32[512,768]{1,0:T(8,128)} %fusion, f32[512,768]{1,0:T(8,128)} %fusion.6, bf16[1,2048,768]{2,1,0:T(8,128)(2,1)} %all-gather.7.cloned.1.call-done, bf16[64,8,2048]{2,1,0:T(8,128)(2,1)S(1)} %all-to-all-done), kind=kOutput, calls=%fused_computation.39 | convolution fusion | flops 1616510976 | bytes 10747904 | tf_op jit(solution)/shard_map/dot_general | solution.py:17
  148.6 0.0 copy-start.7
  148.6 0.0 copy-start.6
  148.6 1.9 fusion.25
  150.5 1.9 fusion.30
  152.5 1.9 fusion.28
  154.4 7.0 %pad_maximum_fusion = f32[2048,2304]{0,1:T(8,128)} fusion(f32[2048,768]{0,1:T(8,128)S(1)} %fusion.25, f32[2048,768]{0,1:T(8,128)S(1)} %fusion.28, f32[2048,768]{0,1:T(8,128)S(1)} %fusion.30), kind=kLoop, calls=%fused_computation.2 | loop fusion | flops 9437184 | bytes 37748736 | tf_op jit(solution)/shard_map/concatenate | solution.py:111
  161.4 0.0 reduce-scatter.2.cloned.1.call-update
  161.4 1.1 copy-done.8
  162.5 5.0 %fusion.19 = bf16[64,8,2048]{2,1,0:T(8,128)(2,1)} fusion(bf16[512,768]{1,0:T(8,128)(2,1)S(1)} %copy-done.8, bf16[1,2048,768]{2,1,0:T(8,128)(2,1)} %all-gather.11.cloned.1.call-done), kind=kOutput, calls=%fused_computation.23 | convolution fusion | flops 1611661312 | bytes 6029312 | tf_op jit(solution)/shard_map/dot_general | solution.py:20
  167.5 10.7 %all-to-all-start.1 = ((bf16[64,8,2048]{2,1,0:T(8,128)(2,1)}), bf16[64,8,2048]{2,1,0:T(8,128)(2,1)S(1)}, u32[]{:S(2)}, u32[]{:S(2)}) async-start(bf16[64,8,2048]{2,1,0:T(8,128)(2,1)} %fusion.19), calls=%async_computation.1 | async-start | bytes 4194304 | tf_op jit(solution)/shard_map/all_to_all | solution.py:75
  178.3 0.0 copy-start.10
  178.3 4.1 %fusion.4 = f32[512,2048]{1,0:T(8,128)S(1)} fusion(bf16[512,768]{1,0:T(8,128)(2,1)} %copy-done.6, bf16[1,2048,768]{2,1,0:T(8,128)(2,1)} %all-gather.9.cloned.1.call-done), kind=kOutput, calls=%fused_computation.9 | convolution fusion | flops 1610612736 | bytes 8126464 | tf_op jit(solution)/shard_map/dot_general | solution.py:36
  182.4 3.2 fusion.22
  185.6 44.0 %all-to-all-done.1 = bf16[64,8,2048]{2,1,0:T(8,128)(2,1)S(1)} async-done(((bf16[64,8,2048]{2,1,0:T(8,128)(2,1)}), bf16[64,8,2048]{2,1,0:T(8,128)(2,1)S(1)}, u32[]{:S(2)}, u32[]{:S(2)}) %all-to-all-start.1) | async-done | bytes 2097184 | tf_op jit(solution)/shard_map/all_to_all | solution.py:75
  229.5 5.6 %all-to-all-start.3 = ((bf16[64,8,2048]{2,1,0:T(8,128)(2,1)}), bf16[64,8,2048]{2,1,0:T(8,128)(2,1)}, u32[]{:S(2)}, u32[]{:S(2)}) async-start(bf16[64,8,2048]{2,1,0:T(8,128)(2,1)} %fusion.22), calls=%async_computation.3 | async-start | bytes 4194304 | tf_op jit(solution)/shard_map/all_to_all | solution.py:87
  235.2 0.1 copy.30
  235.3 0.1 copy.29
  235.4 0.1 reshape.71
  235.5 2.6 mul.79
  238.1 4.7 %mul.80 = f32[384,2048]{1,0:T(8,128)} reshape(f32[64,6,2048]{2,1,0:T(8,128)} %mul.79) | data formatting | bytes 6291456 | tf_op jit(solution)/shard_map/mul | solution.py:96
  242.8 3.1 gather_fusion
  245.9 40.4 %all-to-all-done.3 = bf16[64,8,2048]{2,1,0:T(8,128)(2,1)} async-done(((bf16[64,8,2048]{2,1,0:T(8,128)(2,1)}), bf16[64,8,2048]{2,1,0:T(8,128)(2,1)}, u32[]{:S(2)}, u32[]{:S(2)}) %all-to-all-start.3) | async-done | bytes 2097184 | tf_op jit(solution)/shard_map/all_to_all | solution.py:87
  286.3 7.0 %gather_fusion.1 = bf16[384,2048]{1,0:T(8,128)(2,1)} fusion(bf16[512,2048]{1,0:T(8,128)(2,1)} %bitcast.10, s32[1024]{0:T(1024)S(1)} %pad_clamp_fusion), kind=kCustom, calls=%fused_computation.1.clone | custom fusion | bytes 3147264 | tf_op jit(solution)/shard_map/jit(_take)/gather | solution.py:41
  293.4 3.4 broadcast_select_fusion
  296.8 1.6 reshape.76
  298.4 4.7 %reshape.77 = f32[64,6,2048]{2,1,0:T(8,128)} reshape(f32[384,2048]{1,0:T(8,128)} %get-tuple-element.34) | data formatting | bytes 6291456 | tf_op jit(solution)/shard_map/convert_element_type | solution.py:94
  303.1 2.5 multiply_reduce_fusion.1
  305.6 0.1 reduce_sum.75
  305.7 0.7 copy.31
  306.4 3.7 %reduce_sum.73 = bf16[64,2048]{1,0:T(8,128)(2,1)} reduce(bf16[64,6,2048]{2,1,0:T(8,128)(2,1)} %reshape.76, bf16[]{:T(256)} %constant.26.clone.1), dimensions={1}, to_apply=%region_6.8 | reduce | flops 655360 | bytes 1835010 | tf_op jit(solution)/shard_map/reduce_sum | solution.py:100
  310.1 4.5 %multiply_reduce_fusion = bf16[64,2048]{1,0:T(8,128)(2,1)} fusion(f32[64,6,2048]{2,1,0:T(8,128)} %reshape.77, f32[64,6]{1,0:T(8,128)S(1)} %copy.29), kind=kLoop, calls=%fused_computation.4 | loop fusion | flops 1441792 | bytes 3409408 | tf_op jit(solution)/shard_map/reduce_sum | solution.py:95
  314.6 14.5 %reduce-scatter.2.cloned.1.call-done = f32[512,2304]{0,1:T(8,128)} async-done(((f32[2048,2304]{0,1:T(8,128)}), f32[512,2304]{0,1:T(8,128)}) %reduce-scatter.2.cloned.1.call-update) | async-done | bytes 4718608 | tf_op jit(solution)/shard_map/reduce_scatter | solution.py:110
  329.2 4.0 %slice_bitcast_fusion = (f32[1,512,768]{1,2,0:T(8,128)}, f32[1,512,768]{1,2,0:T(8,128)S(1)}, f32[1,512,768]{1,2,0:T(8,128)S(1)}) fusion(f32[512,2304]{0,1:T(8,128)} %reduce-scatter.2.cloned.1.call-done), kind=kLoop, calls=%fused_computation.34 | loop fusion | bytes 9437184 | tf_op jit(solution)/shard_map/broadcast_in_dim | solution.py:119
  333.2 3.0 copy.34
  336.2 1.6 copy.33
  337.8 1.6 copy.32
  (18 shorter events, 0.1 us)
Async XLA Ops:
  7.2 21.0 %copy-start = (bf16[64,2048]{1,0:T(8,128)(2,1)S(1)}, bf16[64,2048]{1,0:T(8,128)(2,1)}, u32[]{:S(2)}) copy-start(bf16[64,2048]{1,0:T(8,128)(2,1)} %param.9) | copy-start | bytes 786436
  7.2 5.0 %copy-start.5 = (bf16[64,2048]{1,0:T(8,128)(2,1)S(1)}, bf16[64,2048]{1,0:T(8,128)(2,1)}, u32[]{:S(2)}) copy-start(bf16[64,2048]{1,0:T(8,128)(2,1)} %param.12) | copy-start | bytes 786436
  7.2 78.5 %all-gather.11.cloned.1.call-start = ((), (), s32[]{:S(2)}) async-start(), calls=%async_computation.8 | async-start | bytes 3932160 | tf_op jit(solution)/shard_map/all_gather | solution.py:70
  7.9 128.8 %all-gather.9.cloned.1.call-start = ((), (), s32[]{:S(2)}) async-start(), calls=%async_computation.7 | async-start | bytes 3932160 | tf_op jit(solution)/shard_map/all_gather | solution.py:69
  15.4 63.3 %all-to-all-start.2 = ((bf16[64,8,2048]{2,1,0:T(8,128)(2,1)}), bf16[64,8,2048]{2,1,0:T(8,128)(2,1)S(1)}, u32[]{:S(2)}, u32[]{:S(2)}) async-start(bf16[64,8,2048]{2,1,0:T(8,128)(2,1)} %fusion.18), calls=%async_computation.2 | async-start | bytes 4194304 | tf_op jit(solution)/shard_map/all_to_all | solution.py:82
  27.4 115.9 %all-gather.7.cloned.1.call-start = ((), (), s32[]{:S(2)}) async-start(), calls=%async_computation.6 | async-start | bytes 3932160 | tf_op jit(solution)/shard_map/all_gather | solution.py:68
  78.6 1.3 copy-start.3
  80.0 56.7 %all-to-all-start = ((bf16[64,8,2048]{2,1,0:T(8,128)(2,1)}), bf16[64,8,2048]{2,1,0:T(8,128)(2,1)S(1)}, u32[]{:S(2)}, u32[]{:S(2)}) async-start(bf16[64,8,2048]{2,1,0:T(8,128)(2,1)} %fusion.17), calls=%async_computation | async-start | bytes 4194304 | tf_op jit(solution)/shard_map/all_to_all | solution.py:72
  85.4 243.7 %reduce-scatter.2.cloned.1.call-start = ((), (), s32[]{:S(2)}) async-start(), calls=%async_computation.5 | async-start | bytes 23592960 | tf_op jit(solution)/shard_map/reduce_scatter | solution.py:110
  143.3 5.3 %copy-start.4 = (bf16[64,8,2048]{2,1,0:T(8,128)(2,1)S(1)}, bf16[64,8,2048]{2,1,0:T(8,128)(2,1)}, u32[]{:S(2)}) copy-start(bf16[64,8,2048]{2,1,0:T(8,128)(2,1)} %copy-done.3) | copy-start | bytes 6291460
  148.6 2.0 copy-start.7
  148.6 3.9 %copy-start.6 = (bf16[512,768]{1,0:T(8,128)(2,1)}, bf16[512,768]{1,0:T(8,128)(2,1)S(1)}, u32[]{:S(2)}) copy-start(bf16[512,768]{1,0:T(8,128)(2,1)S(1)} %get-tuple-element.31) | copy-start | bytes 2359300
  161.4 1.1 copy-start.8
  167.5 62.0 %all-to-all-start.1 = ((bf16[64,8,2048]{2,1,0:T(8,128)(2,1)}), bf16[64,8,2048]{2,1,0:T(8,128)(2,1)S(1)}, u32[]{:S(2)}, u32[]{:S(2)}) async-start(bf16[64,8,2048]{2,1,0:T(8,128)(2,1)} %fusion.19), calls=%async_computation.1 | async-start | bytes 4194304 | tf_op jit(solution)/shard_map/all_to_all | solution.py:75
  178.3 4.1 %copy-start.10 = (bf16[1,2048,768]{2,1,0:T(8,128)(2,1)S(1)}, bf16[1,2048,768]{2,1,0:T(8,128)(2,1)}, u32[]{:S(2)}) copy-start(bf16[1,2048,768]{2,1,0:T(8,128)(2,1)} %all-gather.7.cloned.1.call-done) | copy-start | bytes 9437188
  185.6 49.7 %copy-start.9 = (f32[64,6]{0,1:T(8,128)S(1)}, f32[64,6]{0,1:T(8,128)}, u32[]{:S(2)}) copy-start(f32[64,6]{0,1:T(8,128)} %param.11) | copy-start | bytes 4612
  229.5 56.8 %all-to-all-start.3 = ((bf16[64,8,2048]{2,1,0:T(8,128)(2,1)}), bf16[64,8,2048]{2,1,0:T(8,128)(2,1)}, u32[]{:S(2)}, u32[]{:S(2)}) async-start(bf16[64,8,2048]{2,1,0:T(8,128)(2,1)} %fusion.22), calls=%async_computation.3 | async-start | bytes 4194304 | tf_op jit(solution)/shard_map/all_to_all | solution.py:87
  286.3 7.0 %copy-start.2 = (bf16[384,2048]{1,0:T(8,128)(2,1)S(1)}, bf16[384,2048]{1,0:T(8,128)(2,1)}, u32[]{:S(2)}) copy-start(bf16[384,2048]{1,0:T(8,128)(2,1)} %gather_fusion) | copy-start | bytes 4718596
  336.2 3.2 copy-start.1
Sparse Core Ops, SparseCore 0:
  9.8 45.0 all-gather.10
  56.8 42.3 all-gather.8
  100.9 42.3 all-gather.6
  161.5 167.5 reduce-scatter.1
where the time goes:
time: 348 us; the launch traced here: 346 us
  waiting for transfers between devices  197 us (57%)
  matrix products  38.9 us (11%)
  local copies, waits for them, and re-layouts  37.6 us (11%)
  starting transfers between devices  34.2 us (10%)
  other arithmetic  24.6 us (7%)
  between operations  14 us (4%)
    all_to_all x1, waiting for transfers between devices, on_device(): lax.all_to_all(grad_send, 'expert', split_axis=0, concat_axis=0, tiled=True)  48.5 us
    all_to_all x1, waiting for transfers between devices, on_device(): lax.all_to_all(row_send, 'expert', split_axis=0, concat_axis=0, tiled=True)  45.5 us
    all_to_all x1, waiting for transfers between devices, on_device(): lax.all_to_all(expert_out.reshape(experts, capacity, model_width), 'exper...  44 us
    all_to_all x1, waiting for transfers between devices, on_device(): lax.all_to_all(d_rows.reshape(experts, capacity, model_width), 'expert',...  40.4 us
    reduce_scatter x1, waiting for transfers between devices, on_device(): lax.psum_scatter(jnp.concatenate([gate_term, up_term, down_term], axis=1)...  14.5 us
    all_to_all x1, starting transfers between devices, on_device(): lax.all_to_all(grad_send, 'expert', split_axis=0, concat_axis=0, tiled=True)  12 us
    all_to_all x1, starting transfers between devices, on_device(): lax.all_to_all(expert_out.reshape(experts, capacity, model_width), 'exper...  10.7 us
    gather x2, local copies, waits for them, and re-layouts, pick_rows(): chosen = jnp.take(source_rows, position.reshape(-1), axis=0)  10.1 us
  transfers between devices with their start and end apart: 8, of which 6 were waited for; matrix products, arithmetic and copies ran while one was open for 20% of the time, Pallas kernels for 0%

commit v1 on v0

--- a/solution.py
+++ b/solution.py
@@ -64,11 +64,11 @@
         .astype(jnp.bfloat16)
         .reshape(experts, capacity, model_width)
     )
-    full_gate, full_up, full_down = (
-        lax.all_gather(gate_proj[0], "dp", axis=0, tiled=True),
-        lax.all_gather(up_proj[0], "dp", axis=0, tiled=True),
-        lax.all_gather(down_proj[0], "dp", axis=0, tiled=True),
+    both = lax.all_gather(
+        jnp.concatenate([gate_proj[0], up_proj[0]], axis=1), "dp", axis=0, tiled=True
     )
+    full_gate, full_up = both[:, : gate_proj.shape[2]], both[:, gate_proj.shape[2] :]
+    full_down = lax.all_gather(down_proj[0], "dp", axis=0, tiled=True)
     rows_in = lax.all_to_all(row_send, "expert", split_axis=0, concat_axis=0, tiled=True)
     rows_flat = rows_in.reshape(-1, model_width)
     expert_out, gate_pre, up_pre, hidden = forward_rows(rows_flat, full_gate, full_up, full_down)
@@ -107,15 +107,17 @@
     down_term = lax.dot_general(
         grads_flat, hidden, contract_rows, preferred_element_type=jnp.float32
     )
+    grad_down = lax.psum_scatter(
+        down_term.astype(jnp.bfloat16), "dp", scatter_dimension=0, tiled=True
+    ).astype(jnp.float32)
     shares = lax.psum_scatter(
-        jnp.concatenate([gate_term, up_term, down_term], axis=1),
+        jnp.concatenate([gate_term, up_term], axis=1).astype(jnp.bfloat16),
         "dp",
         scatter_dimension=0,
         tiled=True,
-    )
+    ).astype(jnp.float32)
     grad_gate = shares[:, :hidden_units]
-    grad_up = shares[:, hidden_units : 2 * hidden_units]
-    grad_down = shares[:, 2 * hidden_units :]
+    grad_up = shares[:, hidden_units:]
     return (mixed, token_grads, prob_grads, grad_gate[None], grad_up[None], grad_down[None])
 
 

time: 348 us -> 317 us (0.911)
  waiting for transfers between devices: 197 us -> 178 us
  local copies, waits for them, and re-layouts: 37.6 us -> 28.5 us
  starting transfers between devices: 34.2 us -> 29.7 us
    reduce_scatter x1 -> x2, waiting for transfers between devices: 14.5 us -> 0.01 us  [the longest x1 0.01 us: on_device(): lax.psum_scatter(down_term.astype(jnp.bfloat16), 'dp', scatter_dimension=...]
    all_to_all x1, starting transfers between devices: 5.43 us -> 12.2 us  [on_device(): lax.all_to_all(row_send, 'expert', split_axis=0, concat_axis=0, tiled=True)]
    all_to_all x1, starting transfers between devices: 12 us -> 5.62 us  [on_device(): lax.all_to_all(grad_send, 'expert', split_axis=0, concat_axis=0, tiled=True)]
    all_to_all x1, waiting for transfers between devices: 40.4 us -> 46.2 us  [on_device(): lax.all_to_all(d_rows.reshape(experts, capacity, model_width), 'expert',...]
    all_to_all x1, waiting for transfers between devices: 48.5 us -> 43.2 us  [on_device(): lax.all_to_all(grad_send, 'expert', split_axis=0, concat_axis=0, tiled=True)]
    all_to_all x1, starting transfers between devices: 10.7 us -> 5.63 us  [on_device(): lax.all_to_all(expert_out.reshape(experts, capacity, model_width), 'exper...]
    unnamed x27 -> x26, local copies, waits for them, and re-layouts: 9.52 us -> 4.93 us
    broadcast_in_dim x1, local copies, waits for them, and re-layouts: 4 us -> 0.31 us  [on_device(): grad_up[None]]
  transfers between devices with their start and end apart: 8 -> 8, of which waited for: 6 -> 4; matrix products, arithmetic and copies ran while one was open for 20% -> 23% of each run, Pallas kernels for 0% -> 0%
where the time goes in v1:
time: 317 us; the launch traced here: 316 us
  waiting for transfers between devices  178 us (56%)
  matrix products  41 us (13%)
  starting transfers between devices  29.7 us (9%)
  local copies, waits for them, and re-layouts  28.5 us (9%)
  other arithmetic  25.4 us (8%)
  between operations  14 us (4%)
    all_to_all x1, waiting for transfers between devices, on_device(): lax.all_to_all(row_send, 'expert', split_axis=0, concat_axis=0, tiled=True)  47.3 us
    all_to_all x1, waiting for transfers between devices, on_device(): lax.all_to_all(d_rows.reshape(experts, capacity, model_width), 'expert',...  46.2 us
    all_to_all x1, waiting for transfers between devices, on_device(): lax.all_to_all(grad_send, 'expert', split_axis=0, concat_axis=0, tiled=True)  43.2 us
    all_to_all x1, waiting for transfers between devices, on_device(): lax.all_to_all(expert_out.reshape(experts, capacity, model_width), 'exper...  40.4 us
    all_to_all x1, starting transfers between devices, on_device(): lax.all_to_all(row_send, 'expert', split_axis=0, concat_axis=0, tiled=True)  12.2 us
    gather x2, local copies, waits for them, and re-layouts, pick_rows(): chosen = jnp.take(source_rows, position.reshape(-1), axis=0)  9.36 us
    mul x2, local copies, waits for them, and re-layouts, on_device(): cotangent.astype(jnp.float32)[:, None, :] * picked  7.33 us
    dot_general x1, matrix products, backward_rows(): d_hidden = jnp.dot(grad_rows, down_proj, preferred_element_type=jnp.float32)  6.5 us
  transfers between devices with their start and end apart: 8, of which 4 were waited for; matrix products, arithmetic and copies ran while one was open for 23% of the time, Pallas kernels for 0%

profile of v1, /device:TPU:2, one launch (start us, length us, event | category | flops | bytes accessed | tf_op | source)
XLA Modules:
  0.0 316.5 jit_solution(14505923415690484897)
XLA Ops:
  7.2 0.0 copy-start
  7.2 0.0 all-gather.4.cloned.1.call-start
  7.2 0.0 copy-start.3
  7.2 0.0 copy-start.4
  7.2 2.7 pad_maximum_fusion.1
  9.9 0.0 all-gather.4.cloned.1.call-update
  9.9 0.0 copy-done.3
  9.9 0.1 convert_reduce_fusion.1
  10.1 0.1 reduce_window_sum.11
  10.2 0.3 select_reduce_fusion.1
  10.5 0.2 select_reduce_fusion
  10.7 2.1 fusion.14
  12.8 12.2 %all-to-all-start = ((bf16[64,8,2048]{2,1,0:T(8,128)(2,1)}), bf16[64,8,2048]{2,1,0:T(8,128)(2,1)S(1)}, u32[]{:S(2)}, u32[]{:S(2)}) async-start(bf16[64,8,2048]{2,1,0:T(8,128)(2,1)} %fusion.14), calls=%async_computation | async-start | bytes 4194304 | tf_op jit(solution)/shard_map/all_to_all | solution.py:72
  24.9 0.0 all-gather.6.cloned.1.call-start
  25.0 0.7 all-gather.6.cloned.1.call-update
  25.7 3.2 %fusion.15 = bf16[64,8,2048]{2,1,0:T(8,128)(2,1)} fusion(f32[512,64]{0,1:T(8,128)S(1)} %get-tuple-element.25, bf16[64,2048]{1,0:T(8,128)(2,1)S(1)} %copy-done.2), kind=kOutput, calls=%fused_computation.24 | convolution fusion | flops 806354944 | bytes 2490368 | tf_op jit(solution)/shard_map/dot_general | solution.py:63
  28.9 47.3 %all-to-all-done = bf16[64,8,2048]{2,1,0:T(8,128)(2,1)S(1)} async-done(((bf16[64,8,2048]{2,1,0:T(8,128)(2,1)}), bf16[64,8,2048]{2,1,0:T(8,128)(2,1)S(1)}, u32[]{:S(2)}, u32[]{:S(2)}) %all-to-all-start) | async-done | bytes 2097184 | tf_op jit(solution)/shard_map/all_to_all | solution.py:72
  76.2 5.6 %all-to-all-start.2 = ((bf16[64,8,2048]{2,1,0:T(8,128)(2,1)}), bf16[64,8,2048]{2,1,0:T(8,128)(2,1)}, u32[]{:S(2)}, u32[]{:S(2)}) async-start(bf16[64,8,2048]{2,1,0:T(8,128)(2,1)} %fusion.15), calls=%async_computation.2 | async-start | bytes 4194304 | tf_op jit(solution)/shard_map/all_to_all | solution.py:82
  81.8 0.0 reduce-scatter.5.cloned.1.call-start
  81.9 0.0 all-gather.4.cloned.1.call-done
  81.9 5.0 %fusion.8 = f32[512,768]{1,0:T(8,128)} fusion(bf16[2048,1536]{1,0:T(8,128)(2,1)} %all-gather.4.cloned.1.call-done, bf16[64,8,2048]{2,1,0:T(8,128)(2,1)S(1)} %all-to-all-done), kind=kOutput, calls=%fused_computation.17 | convolution fusion | flops 1610612736 | bytes 6815744 | tf_op jit(solution)/shard_map/dot_general | solution.py:18
  86.9 2.9 fusion.12
  89.8 43.2 %all-to-all-done.2 = bf16[64,8,2048]{2,1,0:T(8,128)(2,1)} async-done(((bf16[64,8,2048]{2,1,0:T(8,128)(2,1)}), bf16[64,8,2048]{2,1,0:T(8,128)(2,1)}, u32[]{:S(2)}, u32[]{:S(2)}) %all-to-all-start.2) | async-done | bytes 2097184 | tf_op jit(solution)/shard_map/all_to_all | solution.py:82
  133.0 6.5 %multiply_convert_fusion = (bf16[512,768]{1,0:T(8,128)(2,1)S(1)}, bf16[512,768]{1,0:T(8,128)(2,1)}, bf16[512,768]{1,0:T(8,128)(2,1)S(1)}) fusion(f32[512,768]{1,0:T(8,128)} %fusion.12, f32[512,768]{1,0:T(8,128)} %fusion.8, bf16[1,2048,768]{2,1,0:T(8,128)(2,1)} %all-gather.6.cloned.1.call-done, bf16[64,8,2048]{2,1,0:T(8,128)(2,1)} %all-to-all-done.2), kind=kOutput, calls=%fused_computation.37 | convolution fusion | flops 1616510976 | bytes 10747904 | tf_op jit(solution)/shard_map/dot_general | solution.py:27
  139.5 0.9 copy-done.7
  140.4 5.1 %convolution_convert_fusion = bf16[2048,768]{1,0:T(8,128)(2,1)} fusion(bf16[512,768]{1,0:T(8,128)(2,1)S(1)} %get-tuple-element.31, bf16[64,8,2048]{2,1,0:T(8,128)(2,1)} %all-to-all-done.2), kind=kOutput, calls=%fused_computation.5 | convolution fusion | flops 1612185600 | bytes 6029312 | tf_op jit(solution)/shard_map/dot_general | solution.py:107
  145.5 0.0 reduce-scatter.5.cloned.1.call-update
  145.5 0.2 reduce-scatter.3.cloned.1.call-start
  145.7 0.0 copy-start.6
  145.7 1.9 convolution_convert_fusion.1
  147.6 0.0 copy-done.6
  147.6 1.8 convolution_convert_fusion.2
  149.4 3.8 %pad_maximum_fusion = bf16[2048,1536]{0,1:T(8,128)(2,1)} fusion(bf16[2048,768]{0,1:T(8,128)(2,1)S(1)} %convolution_convert_fusion.1, bf16[2048,768]{0,1:T(8,128)(2,1)S(1)} %convolution_convert_fusion.2), kind=kLoop, calls=%fused_computation.2 | loop fusion | flops 12582912 | bytes 12582912 | tf_op jit(solution)/shard_map/concatenate | solution.py:114
  153.2 0.0 reduce-scatter.3.cloned.1.call-update
  153.3 0.0 slice-start.1
  153.3 4.2 %fusion.10 = f32[512,2048]{1,0:T(8,128)S(1)} fusion(bf16[512,768]{1,0:T(8,128)(2,1)} %get-tuple-element.30, bf16[2048,1536]{1,0:T(8,128)(2,1)} %all-gather.4.cloned.1.call-done), kind=kOutput, calls=%fused_computation.19 | convolution fusion | flops 1610612736 | bytes 8126464 | tf_op jit(solution)/shard_map/dot_general | solution.py:35
  157.5 3.2 %fusion.19 = bf16[64,8,2048]{2,1,0:T(8,128)(2,1)} fusion(f32[512,2048]{1,0:T(8,128)S(1)} %fusion.10, bf16[512,768]{1,0:T(8,128)(2,1)S(1)} %get-tuple-element.29, bf16[2048,1536]{1,0:T(8,128)(2,1)S(1)} %bitcast.60), kind=kOutput, calls=%fused_computation.26 | convolution fusion | flops 1612709888 | bytes 10223616 | tf_op jit(solution)/shard_map/dot_general | solution.py:36
  160.8 6.0 %all-to-all-start.3 = ((bf16[64,8,2048]{2,1,0:T(8,128)(2,1)}), bf16[64,8,2048]{2,1,0:T(8,128)(2,1)S(1)}, u32[]{:S(2)}, u32[]{:S(2)}) async-start(bf16[64,8,2048]{2,1,0:T(8,128)(2,1)} %fusion.19), calls=%async_computation.3 | async-start | bytes 4194304 | tf_op jit(solution)/shard_map/all_to_all | solution.py:87
  166.8 0.0 copy-done.8
  166.8 5.1 %fusion.16 = bf16[64,8,2048]{2,1,0:T(8,128)(2,1)} fusion(bf16[512,768]{1,0:T(8,128)(2,1)S(1)} %copy-done.8, bf16[1,2048,768]{2,1,0:T(8,128)(2,1)} %all-gather.6.cloned.1.call-done), kind=kOutput, calls=%fused_computation.25 | convolution fusion | flops 1611661312 | bytes 6029312 | tf_op jit(solution)/shard_map/dot_general | solution.py:20
  171.8 46.2 %all-to-all-done.3 = bf16[64,8,2048]{2,1,0:T(8,128)(2,1)S(1)} async-done(((bf16[64,8,2048]{2,1,0:T(8,128)(2,1)}), bf16[64,8,2048]{2,1,0:T(8,128)(2,1)S(1)}, u32[]{:S(2)}, u32[]{:S(2)}) %all-to-all-start.3) | async-done | bytes 2097184 | tf_op jit(solution)/shard_map/all_to_all | solution.py:87
  218.0 5.6 %all-to-all-start.1 = ((bf16[64,8,2048]{2,1,0:T(8,128)(2,1)}), bf16[64,8,2048]{2,1,0:T(8,128)(2,1)}, u32[]{:S(2)}, u32[]{:S(2)}) async-start(bf16[64,8,2048]{2,1,0:T(8,128)(2,1)} %fusion.16), calls=%async_computation.1 | async-start | bytes 4194304 | tf_op jit(solution)/shard_map/all_to_all | solution.py:75
  223.7 0.1 copy.28
  223.8 0.1 copy.27
  223.9 0.1 reshape.71
  224.0 2.5 mul.79
  226.5 4.8 %mul.80 = f32[384,2048]{1,0:T(8,128)} reshape(f32[64,6,2048]{2,1,0:T(8,128)} %mul.79) | data formatting | bytes 6291456 | tf_op jit(solution)/shard_map/mul | solution.py:96
  231.3 3.1 gather_fusion.1
  234.5 40.4 %all-to-all-done.1 = bf16[64,8,2048]{2,1,0:T(8,128)(2,1)} async-done(((bf16[64,8,2048]{2,1,0:T(8,128)(2,1)}), bf16[64,8,2048]{2,1,0:T(8,128)(2,1)}, u32[]{:S(2)}, u32[]{:S(2)}) %all-to-all-start.1) | async-done | bytes 2097184 | tf_op jit(solution)/shard_map/all_to_all | solution.py:75
  274.8 6.3 %gather_fusion = bf16[384,2048]{1,0:T(8,128)(2,1)S(1)} fusion(bf16[512,2048]{1,0:T(8,128)(2,1)} %bitcast.6, s32[1024]{0:T(1024)S(1)} %pad_clamp_fusion), kind=kCustom, calls=%fused_computation.clone | custom fusion | bytes 3147264 | tf_op jit(solution)/shard_map/jit(_take)/gather | solution.py:41
  281.1 3.5 %broadcast_select_fusion = (bf16[384,2048]{1,0:T(8,128)(2,1)S(1)}, f32[384,2048]{1,0:T(8,128)}) fusion(bf16[384,2048]{1,0:T(8,128)(2,1)} %gather_fusion.1, pred[384]{0:T(512)(128)(4,1)S(1)} %compare_and_fusion, bf16[384,2048]{1,0:T(8,128)(2,1)S(1)} %gather_fusion), kind=kLoop, calls=%fused_computation.42 | loop fusion | flops 2359296 | bytes 7864704 | tf_op jit(solution)/shard_map/jit(_take)/select_n | solution.py:41
  284.6 4.6 %reshape.77 = f32[64,6,2048]{2,1,0:T(8,128)} reshape(f32[384,2048]{1,0:T(8,128)} %get-tuple-element.33) | data formatting | bytes 6291456 | tf_op jit(solution)/shard_map/convert_element_type | solution.py:94
  289.2 1.6 reshape.76
  290.8 2.4 multiply_reduce_fusion.1
  293.2 0.1 reduce_sum.75
  293.4 0.7 copy.29
  294.0 3.6 %reduce_sum.73 = bf16[64,2048]{1,0:T(8,128)(2,1)} reduce(bf16[64,6,2048]{2,1,0:T(8,128)(2,1)} %reshape.76, bf16[]{:T(256)} %constant.26.clone.1), dimensions={1}, to_apply=%region_6.8 | reduce | flops 655360 | bytes 1835010 | tf_op jit(solution)/shard_map/reduce_sum | solution.py:100
  297.7 4.5 %multiply_reduce_fusion = bf16[64,2048]{1,0:T(8,128)(2,1)} fusion(f32[64,6,2048]{2,1,0:T(8,128)} %reshape.77, f32[64,6]{1,0:T(8,128)S(1)} %copy.27), kind=kLoop, calls=%fused_computation.4 | loop fusion | flops 1441792 | bytes 3409408 | tf_op jit(solution)/shard_map/reduce_sum | solution.py:95
  302.1 2.4 bitcast_convert_fusion
  304.5 1.8 convert_element_type.71
  306.4 0.3 slice_bitcast_fusion
  306.7 0.0 copy-start.1
  306.7 1.6 copy.30
  308.3 1.6 copy.31
  (21 shorter events, 0.1 us)
Async XLA Ops:
  7.2 3.5 %copy-start = (bf16[64,2048]{1,0:T(8,128)(2,1)S(1)}, bf16[64,2048]{1,0:T(8,128)(2,1)}, u32[]{:S(2)}) copy-start(bf16[64,2048]{1,0:T(8,128)(2,1)} %param.9) | copy-start | bytes 786436
  7.2 74.7 %all-gather.4.cloned.1.call-start = ((), (), s32[]{:S(2)}) async-start(), calls=%async_computation.6 | async-start | bytes 7864320 | tf_op jit(solution)/shard_map/all_gather | solution.py:67
  7.2 2.7 copy-start.3
  7.2 3.2 %copy-start.4 = (f32[64,6]{0,1:T(8,128)S(1)}, f32[64,6]{0,1:T(8,128)}, u32[]{:S(2)}) copy-start(f32[64,6]{0,1:T(8,128)} %param.11) | copy-start | bytes 4612
  12.8 12.9 %copy-start.2 = (bf16[64,2048]{1,0:T(8,128)(2,1)S(1)}, bf16[64,2048]{1,0:T(8,128)(2,1)}, u32[]{:S(2)}) copy-start(bf16[64,2048]{1,0:T(8,128)(2,1)} %param.12) | copy-start | bytes 786436
  12.8 63.4 %all-to-all-start = ((bf16[64,8,2048]{2,1,0:T(8,128)(2,1)}), bf16[64,8,2048]{2,1,0:T(8,128)(2,1)S(1)}, u32[]{:S(2)}, u32[]{:S(2)}) async-start(bf16[64,8,2048]{2,1,0:T(8,128)(2,1)} %fusion.14), calls=%async_computation | async-start | bytes 4194304 | tf_op jit(solution)/shard_map/all_to_all | solution.py:72
  24.9 108.1 %all-gather.6.cloned.1.call-start = ((), (), s32[]{:S(2)}) async-start(), calls=%async_computation.9 | async-start | bytes 3932160 | tf_op jit(solution)/shard_map/all_gather | solution.py:71
  76.2 56.8 %all-to-all-start.2 = ((bf16[64,8,2048]{2,1,0:T(8,128)(2,1)}), bf16[64,8,2048]{2,1,0:T(8,128)(2,1)}, u32[]{:S(2)}, u32[]{:S(2)}) async-start(bf16[64,8,2048]{2,1,0:T(8,128)(2,1)} %fusion.15), calls=%async_computation.2 | async-start | bytes 4194304 | tf_op jit(solution)/shard_map/all_to_all | solution.py:82
  81.8 220.3 %reduce-scatter.5.cloned.1.call-start = ((), (), s32[]{:S(2)}) async-start(), calls=%async_computation.8 | async-start | bytes 3932160 | tf_op jit(solution)/shard_map/reduce_scatter | solution.py:110
  81.9 5.0 %copy-start.5 = (bf16[2048,1536]{1,0:T(8,128)(2,1)S(1)}, bf16[2048,1536]{1,0:T(8,128)(2,1)}, u32[]{:S(2)}) copy-start(bf16[2048,1536]{1,0:T(8,128)(2,1)} %all-gather.4.cloned.1.call-done) | copy-start | bytes 18874372
  139.5 0.9 copy-start.7
  145.5 159.0 %reduce-scatter.3.cloned.1.call-start = ((), (), s32[]{:S(2)}) async-start(), calls=%async_computation.7 | async-start | bytes 7864320 | tf_op jit(solution)/shard_map/reduce_scatter | solution.py:113
  145.7 1.9 copy-start.6
  153.2 4.3 %slice-start = ((s8[6291456]{0:T(1024)(128)(4,1)}), s8[2097152]{0:T(1024)(128)(4,1)S(1)}, s32[]{:S(2)}) async-start(s8[6291456]{0:T(1024)(128)(4,1)} %bitcast.59), calls=%async_computation.10 | async-start | bytes 4194304
  153.3 4.3 %slice-start.1 = ((s8[6291456]{0:T(1024)(128)(4,1)}), s8[4194304]{0:T(1024)(128)(4,1)S(1)}, s32[]{:S(2)}) async-start(s8[6291456]{0:T(1024)(128)(4,1)} %bitcast.59), calls=%async_computation.11 | async-start | bytes 8388608
  160.8 6.0 %copy-start.8 = (bf16[512,768]{1,0:T(8,128)(2,1)S(1)}, bf16[512,768]{1,0:T(8,128)(2,1)}, u32[]{:S(2)}) copy-start(bf16[512,768]{1,0:T(8,128)(2,1)} %copy-done.7) | copy-start | bytes 2359300
  160.8 57.3 %all-to-all-start.3 = ((bf16[64,8,2048]{2,1,0:T(8,128)(2,1)}), bf16[64,8,2048]{2,1,0:T(8,128)(2,1)S(1)}, u32[]{:S(2)}, u32[]{:S(2)}) async-start(bf16[64,8,2048]{2,1,0:T(8,128)(2,1)} %fusion.19), calls=%async_computation.3 | async-start | bytes 4194304 | tf_op jit(solution)/shard_map/all_to_all | solution.py:87
  218.0 56.8 %all-to-all-start.1 = ((bf16[64,8,2048]{2,1,0:T(8,128)(2,1)}), bf16[64,8,2048]{2,1,0:T(8,128)(2,1)}, u32[]{:S(2)}, u32[]{:S(2)}) async-start(bf16[64,8,2048]{2,1,0:T(8,128)(2,1)} %fusion.16), calls=%async_computation.1 | async-start | bytes 4194304 | tf_op jit(solution)/shard_map/all_to_all | solution.py:75
  306.7 3.2 %copy-start.1 = (bf16[64,2048]{1,0:T(8,128)(2,1)S(1)}, bf16[64,2048]{1,0:T(8,128)(2,1)}, u32[]{:S(2)}) copy-start(bf16[64,2048]{1,0:T(8,128)(2,1)} %param.9) | copy-start | bytes 786436
Sparse Core Ops, SparseCore 0:
  10.4 71.2 all-gather.3
  83.5 42.7 all-gather.5
  145.6 37.1 reduce-scatter.4
  185.2 66.2 reduce-scatter.2

commit v2 on v0

v2 whole, which is shorter than its diff:
```python
import jax
import jax.numpy as jnp
from jax import lax
from jax.experimental import pallas as pl
from jax.experimental.pallas import tpu as pltpu
from jax.sharding import PartitionSpec as P

MESH = pl.DeviceIdType.MESH
BF = jnp.bfloat16
F32 = jnp.float32
NY, NZ, NX, NC = 4, 8, 4, 2
TOK, D, FF, CAP, TOPK = 64, 2048, 768, 8, 6
ROWS = NX * NC * NZ * CAP
GR = 2 * TOK
DY = D // NY
HALF = DY // 2
NT = (((1,), (1,)), ((), ()))
TN = (((0,), (0,)), ((), ()))


def dot(a, b, dims=(((1,), (0,)), ((), ()))):
    return lax.dot_general(a, b, dims, preferred_element_type=F32)


def kernel(
    tok, cot, meta, gw, uw, dw,
    mixed_o, tgrad_o, pg_o, og, ou, od,
    zt, zc, zm, xs_r, xs_g, rows, grads, gu, dn, gp, hid, dgu, xr_o, xr_d,
    pm, wm, zs_o, zr_o, zs_d, zr_d, pgs, pgr, acc_o, acc_d,
    d1, d2, d3, dhp, dhm, dfp, dfm, down,
    g1, g2, g3, ghp, ghm, gfp, gfm, gown,
    ssem, rsem, lsem,
):
    y = lax.axis_index("dp")
    e = lax.axis_index("expert")
    z, x, c = e // (NX * NC), (e // NC) % NX, e % NC

    def at(dy=0, dz=0, dx=0, dc=0):
        return (
            (y + dy + NY) % NY,
            ((z + dz + NZ) % NZ) * (NX * NC) + ((x + dx + NX) % NX) * NC + (c + dc) % NC,
        )

    yp, ym, zp, zq = at(dy=1), at(dy=-1), at(dz=1), at(dz=-1)
    offsets = [(k // NC, k % NC) for k in range(NX * NC)]
    to_x = [at(dx=dx, dc=dc) for dx, dc in offsets]
    from_x = [at(dx=-dx, dc=dc) for dx, dc in offsets]

    barrier = pltpu.get_barrier_semaphore()
    peers = [yp, ym, zp, zq] + to_x[1:]
    for peer in peers:
        pl.semaphore_signal(barrier, inc=1, device_id=peer, device_id_type=MESH)
    pl.semaphore_wait(barrier, len(peers))

    used = [0, 0]
    started = []

    def send(src, dst, peer):
        i = used[0]
        used[0] += 1
        copy = pltpu.make_async_remote_copy(
            src_ref=src, dst_ref=dst, send_sem=ssem.at[i], recv_sem=rsem.at[i],
            device_id=peer, device_id_type=MESH,
        )
        copy.start()
        started.append(copy)
        return copy

    def local(src, dst):
        i = used[1]
        used[1] += 1
        copy = pltpu.make_async_copy(src, dst, lsem.at[i])
        copy.start()
        return copy

    def yrows(dy, start=0, size=DY):
        return pl.ds(pl.multiple_of(((y + dy + NY) % NY) * DY + start, HALF), size)

    gcol, ucol = pl.ds(0, FF), pl.ds(FF, FF)

    def own(w, full, cols):
        dst = full.at[yrows(0), cols]
        return send(w, dst, yp), send(w, dst, ym)

    def relay(pair, full, cols):
        pair[0].wait_recv()
        a = full.at[yrows(-1, 0, HALF), cols]
        first = send(a, a, yp)
        pair[1].wait_recv()
        b = full.at[yrows(1, HALF, HALF), cols]
        return first, send(b, b, ym)

    gate_own = own(gw, gu, gcol)
    up_own = own(uw, gu, ucol)

    def zblock(buf, j, zi, start=0, size=TOK):
        return buf.at[pl.ds(j * GR + zi * TOK + start, size), :]

    def zstep(buf, src, s):
        if s == 0:
            return send(src, zblock(buf, 0, 0), zp), send(src, zblock(buf, 0, 1), zq)
        if s < 3:
            return (
                send(zblock(buf, s - 1, 0), zblock(buf, s, 0), zp),
                send(zblock(buf, s - 1, 1), zblock(buf, s, 1), zq),
            )
        h = TOK // 2
        return (
            send(zblock(buf, 2, 0, 0, h), zblock(buf, 3, 1, 0, h), zp),
            send(zblock(buf, 2, 1, h, h), zblock(buf, 3, 1, h, h), zq),
        )

    def mstep(s):
        if s == 0:
            return send(meta, zm.at[0, 0], zp), send(meta, zm.at[0, 1], zq)
        if s < 3:
            return send(zm.at[s - 1, 0], zm.at[s, 0], zp), send(zm.at[s - 1, 1], zm.at[s, 1], zq)
        return (send(zm.at[2, 0], zm.at[3, 1], zp),)

    m_now = mstep(0)
    t_now = zstep(zt, tok, 0)
    loads = [
        local(gw, gu.at[yrows(0), gcol]),
        local(uw, gu.at[yrows(0), ucol]),
        local(dw, dn.at[yrows(0), :]),
        local(tok, zblock(zt, 3, 0)),
        local(cot, zblock(zc, 3, 0)),
    ]
    zm[3, 0] = meta[...]

    row = lax.broadcasted_iota(jnp.int32, (GR, GR), 0)
    lane = lax.broadcasted_iota(jnp.int32, (GR, GR), 1)
    kk = row >> 4
    expert = (z * (NX * NC) + (((x + (kk >> 1)) & (NX - 1)) << 1) + ((c + kk) & 1)).astype(F32)
    slot = (row & (CAP - 1)).astype(F32)
    same_block = ((row >> 3) & 1) == (lane >> 6)
    earlier = jnp.where(((row >> 6) == (lane >> 6)) & (row < lane), 1.0, 0.0).astype(BF)
    low = lax.broadcasted_iota(jnp.int32, (16, GR), 1) < TOK

    def joined(j):
        return jnp.where(low, zm[j, 0], zm[j, 1])

    def route(j):
        both = joined(j)
        named = jnp.zeros((GR, GR), F32)
        weight = jnp.zeros((GR, GR), F32)
        for i in range(TOPK):
            hit = both[i : i + 1, :] == expert
            named = jnp.where(hit, 1.0, named)
            weight = weight + jnp.where(hit, both[8 + i : 9 + i, :], 0.0)
        rank = dot(named.astype(BF), earlier)
        fits = (named > 0.5) & (rank == slot) & same_block
        pm[j] = jnp.where(fits, 1.0, 0.0).astype(BF)
        wm[j] = jnp.where(fits, weight, 0.0)

    def group(buf, j):
        return buf.at[pl.ds(j * GR, GR), :]

    def piece(buf, j, k):
        return buf.at[pl.ds(j * GR + k * 16, 16), :]

    def xsend(src, dst, j, targets):
        return [send(piece(src, j, k), piece(dst, j, k), targets[k]) for k in range(1, NX * NC)]

    dispatched = []

    def dispatch_rows(j):
        filled = dot(pm[j], group(zt, j)[...]).astype(BF)
        group(xs_r, j)[...] = filled
        piece(rows, j, 0)[...] = filled[:16]
        dispatched.extend(xsend(xs_r, rows, j, to_x))

    def dispatch_grads(j):
        prob = jnp.sum(wm[j], axis=1, keepdims=True)
        filled = (dot(pm[j], group(zc, j)[...]) * prob).astype(BF)
        group(xs_g, j)[...] = filled
        piece(grads, j, 0)[...] = filled[:16]
        dispatched.extend(xsend(xs_g, grads, j, to_x))

    c_now = None
    gate_far = up_far = down_own = None
    for s in range(1, 5):
        t_next = m_next = None
        for copy in m_now:
            copy.wait_recv()
        if s < 4:
            m_now = mstep(s)
        for copy in t_now:
            copy.wait_recv()
        if s < 4:
            t_now = zstep(zt, tok, s)
        if s == 3:
            gate_far = relay(gate_own, gu, gcol)
        if s == 3:
            c_now = zstep(zc, cot, 0)
        if s == 4:
            loads[3].wait()
        route(s - 1)
        dispatch_rows(s - 1)
    loads[4].wait()
    for s in range(1, 5):
        for copy in c_now:
            copy.wait_recv()
        if s < 4:
            c_now = zstep(zc, cot, s)
        if s == 3:
            up_far = relay(up_own, gu, ucol)
            down_own = own(dw, dn, slice(None))
        dispatch_grads(s - 1)

    for copy in loads[:3]:
        copy.wait()
    for copy in dispatched[: 4 * 7]:
        copy.wait_recv()
    for copy in gate_far + up_far:
        copy.wait_recv()

    def forward_tile(n, carry):
        a = pl.ds(pl.multiple_of(n * 256, 256), 256)
        b = pl.ds(pl.multiple_of(n * 256 + FF, 256), 256)
        gate_pre = dot(rows[...], gu[:, a])
        gp[:, a] = gate_pre
        up_pre = dot(rows[...], gu[:, b])
        gp[:, b] = up_pre
        hid[:, a] = (gate_pre * (1.0 / (1.0 + jnp.exp(-gate_pre))) * up_pre).astype(BF)
        return carry

    lax.fori_loop(0, FF // 256, forward_tile, 0)
    for copy in dispatched[4 * 7 :]:
        copy.wait_recv()

    def term(src, rhs, dy, store):
        def tile(i, carry):
            cols = pl.ds(pl.multiple_of(((y + dy + NY) % NY) * DY + i * 256, 256), 256)
            store(pl.ds(pl.multiple_of(i * 256, 256), 256), dot(src[:, cols], rhs[...], TN))
            return carry

        lax.fori_loop(0, DY // 256, tile, 0)

    def into(buf):
        def store(where, value):
            buf[where, :] = value.astype(buf.dtype)

        return store

    lo, hi = pl.ds(0, HALF), pl.ds(HALF, HALF)

    def shares(src, rhs, s1, s2, s3, hp, hm, fp, fm, mine):
        term(src, rhs, 2, into(s2))
        half_p = send(s2.at[lo, :], hp, yp)
        half_m = send(s2.at[hi, :], hm, ym)
        term(src, rhs, 1, into(s1))
        last = [send(s1.at[hi, :], fp.at[hi, :], yp)]
        term(src, rhs, -1, into(s3))
        last.append(send(s3.at[lo, :], fm.at[lo, :], ym))
        term(src, rhs, 0, into(mine))
        return half_p, half_m, last

    def pass_on(state, s1, s3, hp, hm, fp, fm):
        half_p, half_m, last = state
        half_p.wait_recv()

        def add_p(i, carry):
            r = pl.ds(pl.multiple_of(i * 64, 64), 64)
            s1[r, :] = (s1[r, :].astype(F32) + hp[r, :].astype(F32)).astype(BF)
            return carry

        lax.fori_loop(0, HALF // 64, add_p, 0)
        last.append(send(s1.at[lo, :], fp.at[lo, :], yp))
        half_m.wait_recv()

        def add_m(i, carry):
            r = pl.ds(pl.multiple_of(i * 64, 64), 64)
            t = pl.ds(pl.multiple_of(i * 64 + HALF, 64), 64)
            s3[t, :] = (s3[t, :].astype(F32) + hm[r, :].astype(F32)).astype(BF)
            return carry

        lax.fori_loop(0, HALF // 64, add_m, 0)
        last.append(send(s3.at[hi, :], fm.at[hi, :], ym))
        return last

    def finish(last, mine, fp, fm):
        for copy in last:
            copy.wait_recv()

        def add(i, carry):
            r = pl.ds(pl.multiple_of(i * 64, 64), 64)
            mine[r, :] = mine[r, :] + fp[r, :].astype(F32) + fm[r, :].astype(F32)
            return carry

        lax.fori_loop(0, DY // 64, add, 0)

    down_far = relay(down_own, dn, slice(None))
    down_state = shares(grads, hid, d1, d2, d3, dhp, dhm, dfp, dfm, down)
    for copy in down_far:
        copy.wait_recv()
    for copy in dispatched:
        copy.wait_send()

    def out_tile(n, carry):
        a = pl.ds(pl.multiple_of(n * 256, 256), 256)
        xs_r[:, a] = dot(hid[...], dn[a, :], NT).astype(BF)
        return carry

    lax.fori_loop(0, D // 256, out_tile, 0)
    back_o = {}
    for j in (3, 2, 1, 0):
        back_o[j] = xsend(xs_r, xr_o, j, from_x)
        piece(xr_o, j, 0)[...] = piece(xs_r, j, 0)[...]

    def backward_tile(n, carry):
        a = pl.ds(pl.multiple_of(n * 256, 256), 256)
        b = pl.ds(pl.multiple_of(n * 256 + FF, 256), 256)
        d_hidden = dot(grads[...], dn[:, a])
        gate_pre = gp[:, a]
        q = 1.0 / (1.0 + jnp.exp(-gate_pre))
        dgu[:, a] = (d_hidden * gp[:, b] * q * (1.0 + gate_pre * (1.0 - q))).astype(BF)
        dgu[:, b] = (d_hidden * (gate_pre * q)).astype(BF)
        return carry

    lax.fori_loop(0, FF // 256, backward_tile, 0)
    down_last = pass_on(down_state, d1, d3, dhp, dhm, dfp, dfm)
    gu_state = shares(rows, dgu, g1, g2, g3, ghp, ghm, gfp, gfm, gown)

    def d_rows_tile(n, carry):
        a = pl.ds(pl.multiple_of(n * 256, 256), 256)
        xs_g[:, a] = dot(dgu[...], gu[a, :], NT).astype(BF)
        return carry

    lax.fori_loop(0, D // 256, d_rows_tile, 0)
    back_d = {}
    for j in (3, 2, 1, 0):
        back_d[j] = xsend(xs_g, xr_d, j, from_x)
        piece(xr_d, j, 0)[...] = piece(xs_g, j, 0)[...]

    def ring(q, part, zs, zr, acc, prev):
        h = TOK // 2
        if q == 0:
            acc[...] = part[:TOK]
            zs[0, 0, :h] = part[TOK : TOK + h].astype(BF)
            zs[1, 0, :h] = part[TOK + h :].astype(BF)
            return (
                send(zs.at[0, 0, pl.ds(0, h)], zr.at[0, 0, pl.ds(0, h)], zp),
                send(zs.at[1, 0, pl.ds(0, h)], zr.at[1, 0, pl.ds(0, h)], zq),
            )
        p0, p1 = part[:TOK], part[TOK:]
        prev[0].wait_recv()
        if q == 1:
            zs[0, q, :h] = (p1[:h] + zr[0, 0, :h].astype(F32)).astype(BF)
            zs[0, q, h:] = p1[h:].astype(BF)
        else:
            zs[0, q] = (p1 + zr[0, q - 1].astype(F32)).astype(BF)
        first = send(zs.at[0, q], zr.at[0, q], zp)
        prev[1].wait_recv()
        if q == 1:
            zs[1, q, h:] = (p0[h:] + zr[1, 0, :h].astype(F32)).astype(BF)
            zs[1, q, :h] = p0[:h].astype(BF)
        else:
            zs[1, q] = (p0 + zr[1, q - 1].astype(F32)).astype(BF)
        return first, send(zs.at[1, q], zr.at[1, q], zq)

    def ring_small(q, part, prev):
        if q == 0:
            pgs[1, 0] = part
            pgs[0, 0] = part
            return (send(pgs.at[0, 0], pgr.at[0, 0], zp),)
        prev[0].wait_recv()
        pgs[0, q] = part + pgr[0, q - 1]
        first = send(pgs.at[0, q], pgr.at[0, q], zp)
        if q == 1:
            pgs[1, q] = part
        else:
            prev[1].wait_recv()
            pgs[1, q] = part + pgr[1, q - 1]
        return first, send(pgs.at[1, q], pgr.at[1, q], zq)

    ring_o = ring_p = ring_d = None
    for q in range(4):
        j = 3 - q
        for copy in back_o[j]:
            copy.wait_recv()
        returned = group(xr_o, j)[...]
        w = wm[j]
        w_hi = w.astype(BF)
        w_lo = (w - w_hi.astype(F32)).astype(BF)
        part = dot(w_hi, returned, TN) + dot(w_lo, returned, TN)
        ring_o = ring(q, part, zs_o, zr_o, acc_o, ring_o)
        scores = dot(returned, group(zc, j)[...], NT) * pm[j].astype(F32)
        both = joined(j)
        small = [
            jnp.sum(jnp.where(both[i : i + 1, :] == expert, scores, 0.0), axis=0, keepdims=True)
            for i in range(TOPK)
        ]
        small = jnp.concatenate(small + [jnp.zeros((2, GR), F32)], axis=0)
        ring_p = ring_small(q, small, ring_p)
    gu_last = pass_on(gu_state, g1, g3, ghp, ghm, gfp, gfm)
    for q in range(4):
        j = 3 - q
        for copy in back_d[j]:
            copy.wait_recv()
        part = dot(pm[j], group(xr_d, j)[...], TN)
        ring_d = ring(q, part, zs_d, zr_d, acc_d, ring_d)

    for copy in ring_o + ring_p:
        copy.wait_recv()
    mixed_o[...] = (acc_o[...] + zr_o[0, 3].astype(F32) + zr_o[1, 3].astype(F32)).astype(BF)
    pg_o[...] = pgs[1, 0] + pgr[1, 3] + pltpu.roll(pgr[0, 3], TOK, 1)
    finish(down_last, down, dfp, dfm)
    stores = [local(down, od)]
    for copy in ring_d:
        copy.wait_recv()
    tgrad_o[...] = (acc_d[...] + zr_d[0, 3].astype(F32) + zr_d[1, 3].astype(F32)).astype(BF)
    finish(gu_last, gown, gfp, gfm)
    stores.append(local(gown.at[:, gcol], og))
    stores.append(local(gown.at[:, ucol], ou))
    for copy in started:
        if not any(copy is other for other in dispatched):
            copy.wait_send()
    for copy in stores:
        copy.wait()


def layer(tokens, expert_ids, gate_probs, cotangent, gate_proj, up_proj, down_proj):
    ids = jnp.pad(expert_ids.T.astype(F32), ((0, 8 - TOPK), (0, 0)), constant_values=-1.0)
    probs = jnp.pad(gate_probs.T, ((0, 8 - TOPK), (0, 0)))
    meta = jnp.tile(jnp.concatenate([ids, probs], axis=0), (1, 2))
    vmem = pl.BlockSpec(memory_space=pltpu.VMEM)
    anywhere = pl.BlockSpec(memory_space=pl.ANY)
    v = pltpu.VMEM
    block = [v((DY, FF), BF)] * 3 + [v((HALF, FF), BF)] * 2 + [v((DY, FF), BF)] * 2
    wide = [v((DY, 2 * FF), BF)] * 3 + [v((HALF, 2 * FF), BF)] * 2 + [v((DY, 2 * FF), BF)] * 2
    scratch = [
        v((4 * GR, D), BF), v((4 * GR, D), BF), v((4, 2, 16, GR), F32),
        v((ROWS, D), BF), v((ROWS, D), BF), v((ROWS, D), BF), v((ROWS, D), BF),
        v((D, 2 * FF), BF), v((D, FF), BF),
        v((ROWS, 2 * FF), F32), v((ROWS, FF), BF), v((ROWS, 2 * FF), BF),
        v((ROWS, D), BF), v((ROWS, D), BF),
        v((4, GR, GR), BF), v((4, GR, GR), F32),
        v((2, 4, TOK, D), BF), v((2, 4, TOK, D), BF), v((2, 4, TOK, D), BF), v((2, 4, TOK, D), BF),
        v((2, 4, 8, GR), F32), v((2, 4, 8, GR), F32), v((TOK, D), F32), v((TOK, D), F32),
        *block, v((DY, FF), F32), *wide, v((DY, 2 * FF), F32),
        pltpu.SemaphoreType.DMA((192,)), pltpu.SemaphoreType.DMA((192,)), pltpu.SemaphoreType.DMA((8,)),
    ]
    grad = jax.ShapeDtypeStruct((DY, FF), F32)
    mixed, token_grads, prob_grads, grad_gate, grad_up, grad_down = pl.pallas_call(
        kernel,
        out_shape=(
            jax.ShapeDtypeStruct((TOK, D), BF),
            jax.ShapeDtypeStruct((TOK, D), BF),
            jax.ShapeDtypeStruct((8, GR), F32),
            grad, grad, grad,
        ),
        in_specs=[vmem] * 3 + [anywhere] * 3,
        out_specs=(vmem,) * 3 + (anywhere,) * 3,
        scratch_shapes=scratch,
        name="expert_layer",
        compiler_params=pltpu.CompilerParams(
            collective_id=0, has_side_effects=True, vmem_limit_bytes=67043328
        ),
    )(tokens, cotangent, meta, gate_proj[0], up_proj[0], down_proj[0])
    return (
        mixed, token_grads, prob_grads[:TOPK, :TOK].T,
        grad_gate[None], grad_up[None], grad_down[None],
    )


def solution(mesh):
    rows, weights = P(("dp", "expert"), None), P("expert", "dp", None)
    return jax.shard_map(
        layer,
        mesh=mesh,
        in_specs=(rows,) * 4 + (weights,) * 3,
        out_specs=(rows,) * 3 + (weights,) * 3,
        check_vma=False,
    )
```

time: 348 us -> 183 us (0.53)
  waiting for transfers between devices: 197 us -> 0 us
  Pallas kernels: 0 us -> 169 us
  matrix products: 38.9 us -> 0 us
  starting transfers between devices: 34.2 us -> 0 us
  local copies, waits for them, and re-layouts: 37.6 us -> 11.2 us
  other arithmetic: 24.6 us -> 1.38 us
  between operations: 14 us -> 0.65 us
    all_to_all x4 -> x0, waiting for transfers between devices: 178 us -> none  [the longest x1 48.5 us: on_device(): lax.all_to_all(grad_send, 'expert', split_axis=0, concat_axis=0, tiled=True)]
    pallas_call x0 -> x1, Pallas kernels: none -> 169 us  [layer(): pl.pallas_call(kernel, out_shape=(jax.ShapeDtypeStruct((TOK, D), BF), jax...]
    dot_general x11 -> x0, matrix products: 38.9 us -> none  [the longest x1 5.49 us: backward_rows(): d_hidden = jnp.dot(grad_rows, down_proj, preferred_element_type=jnp.float32)]
    all_to_all x4 -> x0, starting transfers between devices: 33.8 us -> none  [the longest x1 12 us: on_device(): lax.all_to_all(grad_send, 'expert', split_axis=0, concat_axis=0, tiled=True)]
    reduce_scatter x1 -> x0, waiting for transfers between devices: 14.5 us -> none  [on_device(): lax.psum_scatter(jnp.concatenate([gate_term, up_term, down_term], axis=1)...]
    reduce_sum x6 -> x0, other arithmetic: 13.4 us -> none  [the longest x1 4.51 us: on_device(): jnp.sum(gate_probs[:, :, None] * picked, axis=1).astype(jnp.bfloat16)]
    gather x2 -> x0, local copies, waits for them, and re-layouts: 10.1 us -> none  [pick_rows(): chosen = jnp.take(source_rows, position.reshape(-1), axis=0)]
    mul x2 -> x0, local copies, waits for them, and re-layouts: 7.31 us -> none  [on_device(): cotangent.astype(jnp.float32)[:, None, :] * picked]
  transfers between devices with their start and end apart: 8 -> 0, of which waited for: 6 -> 0; matrix products, arithmetic and copies ran while one was open for 20% -> 0% of each run, Pallas kernels for 0% -> 0%
where the time goes in v2:
time: 183 us; the launch traced here: 182 us
  Pallas kernels  169 us (92%)
  local copies, waits for them, and re-layouts  11.2 us (6%)
    pallas_call x1, Pallas kernels, layer(): pl.pallas_call(kernel, out_shape=(jax.ShapeDtypeStruct((TOK, D), BF), jax...  169 us
    unnamed x9, local copies, waits for them, and re-layouts  9.23 us

profile of v2, /device:TPU:2, one launch (start us, length us, event | category | flops | bytes accessed | tf_op | source)
XLA Modules:
  0.0 182.0 jit_solution(18400702572877727422)
XLA Ops:
  0.6 0.7 convert_bitcast_fusion
  1.3 0.7 select_maximum_fusion
  2.0 0.7 tile.10.meta
  2.7 168.8 %expert_layer.1 = (bf16[64,2048]{1,0:T(8,128)(2,1)}, bf16[64,2048]{1,0:T(8,128)(2,1)}, f32[8,128]{1,0:T(8,128)}, f32[512,768]{1,0:T(8,128)}, f32[512,768]{1,0:T(8,128)}, /*index=5*/f32[512,768]{1,0:T(8,128)}) custom-call(bf16[64,2048]{1,0:T(8,128)(2,1)} %tok.1, bf16[64,2048]{1,0:T(8,128)(2,1)} %cot.1, f32[16,128]{1,0:T(8,128)} %tile.10.meta, ...), custom_call_target="tpu_custom_call" | custom-call | tf_op jit(solution)/shard_map/expert_layer/pallas_call | solution.py:445
  171.5 1.3 slice_bitcast_fusion
  172.8 1.7 copy.18
  174.4 1.7 copy.19
  176.1 0.0 copy-start.1
  176.1 2.8 %copy.20 = f32[1,512,768]{2,1,0:T(8,128)} copy(f32[1,512,768]{2,1,0:T(8,128)} %bitcast.13) | data formatting | bytes 3145728
  178.9 0.0 copy-done.1
  178.9 0.0 copy-start
  178.9 1.1 copy.21
  180.0 0.8 copy-done
  180.8 1.1 copy.22
  (1 shorter events, 0.0 us)
Async XLA Ops:
  176.1 2.8 %copy-start.1 = (f32[512,768]{1,0:T(8,128)S(1)}, f32[512,768]{1,0:T(8,128)}, u32[]{:S(2)}) copy-start(f32[512,768]{1,0:T(8,128)} %get-tuple-element.16) | copy-start | bytes 4718596
  178.9 2.0 %copy-start = (f32[512,768]{1,0:T(8,128)S(1)}, f32[512,768]{1,0:T(8,128)}, u32[]{:S(2)}) copy-start(f32[512,768]{1,0:T(8,128)} %get-tuple-element.17) | copy-start | bytes 4718596

commit v3 on v2

--- a/solution.py
+++ b/solution.py
@@ -16,6 +16,7 @@
 HALF = DY // 2
 NT = (((1,), (1,)), ((), ()))
 TN = (((0,), (0,)), ((), ()))
+VMEM_LIMIT = 57 * 1024 * 1024
 
 
 def dot(a, b, dims=(((1,), (0,)), ((), ()))):
@@ -23,12 +24,12 @@
 
 
 def kernel(
-    tok, cot, meta, gw, uw, dw,
+    tok, cot, ids, probs, gw, uw, dw,
     mixed_o, tgrad_o, pg_o, og, ou, od,
     zt, zc, zm, xs_r, xs_g, rows, grads, gu, dn, gp, hid, dgu, xr_o, xr_d,
-    pm, wm, zs_o, zr_o, zs_d, zr_d, pgs, pgr, acc_o, acc_d,
-    d1, d2, d3, dhp, dhm, dfp, dfm, down,
-    g1, g2, g3, ghp, ghm, gfp, gfm, gown,
+    meta, pm, wm, zs_o, zr_o, zs_d, zr_d, pgs, pgr, acc_o, acc_d,
+    d1, d2, d3, dhp, dhm, dfp, dfm,
+    g1, g2, g3, ghp, ghm, gfp, gfm,
     ssem, rsem, lsem,
 ):
     y = lax.axis_index("dp")
@@ -78,17 +79,24 @@
 
     gcol, ucol = pl.ds(0, FF), pl.ds(FF, FF)
 
+    lo, hi = pl.ds(0, HALF), pl.ds(HALF, HALF)
+
     def own(w, full, cols):
-        dst = full.at[yrows(0), cols]
-        return send(w, dst, yp), send(w, dst, ym)
-
-    def relay(pair, full, cols):
-        pair[0].wait_recv()
+        first, second = full.at[yrows(0, 0, HALF), cols], full.at[yrows(0, HALF, HALF), cols]
+        return (
+            send(w.at[lo, :], first, yp),
+            send(w.at[hi, :], second, ym),
+            send(w.at[hi, :], second, yp),
+            send(w.at[lo, :], first, ym),
+        )
+
+    def relay(parts, full, cols):
+        parts[0].wait_recv()
         a = full.at[yrows(-1, 0, HALF), cols]
         first = send(a, a, yp)
-        pair[1].wait_recv()
+        parts[1].wait_recv()
         b = full.at[yrows(1, HALF, HALF), cols]
-        return first, send(b, b, ym)
+        return first, send(b, b, ym), parts[2], parts[3]
 
     gate_own = own(gw, gu, gcol)
     up_own = own(uw, gu, ucol)
@@ -117,6 +125,10 @@
             return send(zm.at[s - 1, 0], zm.at[s, 0], zp), send(zm.at[s - 1, 1], zm.at[s, 1], zq)
         return (send(zm.at[2, 0], zm.at[3, 1], zp),)
 
+    meta[...] = jnp.full(meta.shape, -1.0, F32)
+    for start in (0, TOK):
+        meta[0:TOPK, start : start + TOK] = ids[...].astype(F32)
+        meta[8 : 8 + TOPK, start : start + TOK] = probs[...]
     m_now = mstep(0)
     t_now = zstep(zt, tok, 0)
     loads = [
@@ -243,55 +255,69 @@
 
         return store
 
-    lo, hi = pl.ds(0, HALF), pl.ds(HALF, HALF)
-
     def shares(src, rhs, s1, s2, s3, hp, hm, fp, fm, mine):
         term(src, rhs, 2, into(s2))
         half_p = send(s2.at[lo, :], hp, yp)
         half_m = send(s2.at[hi, :], hm, ym)
         term(src, rhs, 1, into(s1))
-        last = [send(s1.at[hi, :], fp.at[hi, :], yp)]
+        early = [send(s1.at[hi, :], fp.at[hi, :], yp)]
         term(src, rhs, -1, into(s3))
-        last.append(send(s3.at[lo, :], fm.at[lo, :], ym))
-        term(src, rhs, 0, into(mine))
-        return half_p, half_m, last
-
-    def pass_on(state, s1, s3, hp, hm, fp, fm):
-        half_p, half_m, last = state
-        half_p.wait_recv()
-
-        def add_p(i, carry):
-            r = pl.ds(pl.multiple_of(i * 64, 64), 64)
-            s1[r, :] = (s1[r, :].astype(F32) + hp[r, :].astype(F32)).astype(BF)
-            return carry
-
-        lax.fori_loop(0, HALF // 64, add_p, 0)
-        last.append(send(s1.at[lo, :], fp.at[lo, :], yp))
-        half_m.wait_recv()
-
-        def add_m(i, carry):
-            r = pl.ds(pl.multiple_of(i * 64, 64), 64)
-            t = pl.ds(pl.multiple_of(i * 64 + HALF, 64), 64)
-            s3[t, :] = (s3[t, :].astype(F32) + hm[r, :].astype(F32)).astype(BF)
-            return carry
-
-        lax.fori_loop(0, HALF // 64, add_m, 0)
-        last.append(send(s3.at[hi, :], fm.at[hi, :], ym))
-        return last
-
-    def finish(last, mine, fp, fm):
-        for copy in last:
+        early.append(send(s3.at[lo, :], fm.at[lo, :], ym))
+        term(src, rhs, 0, mine)
+        return half_p, half_m, early
+
+    def pass_on(state, s1, s3, hp, hm, fp, fm, cuts):
+        half_p, half_m, early = state
+        late = []
+        for n, (start, size) in enumerate(cuts):
+            cols = pl.ds(start, size)
+            if n == 0:
+                half_p.wait_recv()
+
+            def add_p(i, carry, cols=cols):
+                r = pl.ds(pl.multiple_of(i * 64, 64), 64)
+                s1[r, cols] = (s1[r, cols].astype(F32) + hp[r, cols].astype(F32)).astype(BF)
+                return carry
+
+            lax.fori_loop(0, HALF // 64, add_p, 0)
+            first = send(s1.at[lo, cols], fp.at[lo, cols], yp)
+            if n == 0:
+                half_m.wait_recv()
+
+            def add_m(i, carry, cols=cols):
+                r = pl.ds(pl.multiple_of(i * 64, 64), 64)
+                t = pl.ds(pl.multiple_of(i * 64 + HALF, 64), 64)
+                s3[t, cols] = (s3[t, cols].astype(F32) + hm[r, cols].astype(F32)).astype(BF)
+                return carry
+
+            lax.fori_loop(0, HALF // 64, add_m, 0)
+            late.append((first, send(s3.at[hi, cols], fm.at[hi, cols], ym)))
+        return early, late
+
+    def finish(sent, cuts, fp, fm, outs):
+        early, late = sent
+        for copy in early:
             copy.wait_recv()
-
-        def add(i, carry):
-            r = pl.ds(pl.multiple_of(i * 64, 64), 64)
-            mine[r, :] = mine[r, :] + fp[r, :].astype(F32) + fm[r, :].astype(F32)
-            return carry
-
-        lax.fori_loop(0, DY // 64, add, 0)
+        for (start, size), pair, (out, at_col) in zip(cuts, late, outs):
+            cols, mine = pl.ds(start, size), pl.ds(at_col, size)
+            for copy in pair:
+                copy.wait_recv()
+
+            def add(i, carry, cols=cols, mine=mine, out=out):
+                r = pl.ds(pl.multiple_of(i * 64, 64), 64)
+                out[r, mine] = out[r, mine] + fp[r, cols].astype(F32) + fm[r, cols].astype(F32)
+                return carry
+
+            lax.fori_loop(0, DY // 64, add, 0)
+
+    def gate_up(where, value):
+        og[where, :] = value[:, :FF]
+        ou[where, :] = value[:, FF:]
+
+    down_cuts, gu_cuts = ((0, FF),), ((0, FF), (FF, 512), (FF + 512, 256))
 
     down_far = relay(down_own, dn, slice(None))
-    down_state = shares(grads, hid, d1, d2, d3, dhp, dhm, dfp, dfm, down)
+    down_state = shares(grads, hid, d1, d2, d3, dhp, dhm, dfp, dfm, into(od))
     for copy in down_far:
         copy.wait_recv()
     for copy in dispatched:
@@ -319,8 +345,8 @@
         return carry
 
     lax.fori_loop(0, FF // 256, backward_tile, 0)
-    down_last = pass_on(down_state, d1, d3, dhp, dhm, dfp, dfm)
-    gu_state = shares(rows, dgu, g1, g2, g3, ghp, ghm, gfp, gfm, gown)
+    down_last = pass_on(down_state, d1, d3, dhp, dhm, dfp, dfm, down_cuts)
+    gu_state = shares(rows, dgu, g1, g2, g3, ghp, ghm, gfp, gfm, gate_up)
 
     def d_rows_tile(n, carry):
         a = pl.ds(pl.multiple_of(n * 256, 256), 256)
@@ -393,7 +419,7 @@
         ]
         small = jnp.concatenate(small + [jnp.zeros((2, GR), F32)], axis=0)
         ring_p = ring_small(q, small, ring_p)
-    gu_last = pass_on(gu_state, g1, g3, ghp, ghm, gfp, gfm)
+    gu_last = pass_on(gu_state, g1, g3, ghp, ghm, gfp, gfm, gu_cuts)
     for q in range(4):
         j = 3 - q
         for copy in back_d[j]:
@@ -405,25 +431,33 @@
         copy.wait_recv()
     mixed_o[...] = (acc_o[...] + zr_o[0, 3].astype(F32) + zr_o[1, 3].astype(F32)).astype(BF)
     pg_o[...] = pgs[1, 0] + pgr[1, 3] + pltpu.roll(pgr[0, 3], TOK, 1)
-    finish(down_last, down, dfp, dfm)
-    stores = [local(down, od)]
+    finish(down_last, down_cuts, dfp, dfm, ((od, 0),))
     for copy in ring_d:
         copy.wait_recv()
     tgrad_o[...] = (acc_d[...] + zr_d[0, 3].astype(F32) + zr_d[1, 3].astype(F32)).astype(BF)
-    finish(gu_last, gown, gfp, gfm)
-    stores.append(local(gown.at[:, gcol], og))
-    stores.append(local(gown.at[:, ucol], ou))
     for copy in started:
-        if not any(copy is other for other in dispatched):
+        if not any(copy is other for other in dispatched + list(gu_late(gu_last))):
             copy.wait_send()
-    for copy in stores:
+    finish(gu_last, gu_cuts, gfp, gfm, ((og, 0), (ou, 0), (ou, 512)))
+    for copy in gu_late(gu_last):
+        copy.wait_send()
+
+
+def gu_late(sent):
+    return [copy for pair in sent[1] for copy in pair]
+
+
+def write_out(mixed, tgrad, pg, g, u, d, mixed_o, tgrad_o, pg_o, og, ou, od, sem):
+    pairs = ((g, og), (u, ou), (d, od), (mixed, mixed_o), (tgrad, tgrad_o))
+    copies = [pltpu.make_async_copy(src, dst, sem.at[i]) for i, (src, dst) in enumerate(pairs)]
+    for copy in copies:
+        copy.start()
+    pg_o[...] = pg[:TOPK, :TOK]
+    for copy in copies:
         copy.wait()
 
 
 def layer(tokens, expert_ids, gate_probs, cotangent, gate_proj, up_proj, down_proj):
-    ids = jnp.pad(expert_ids.T.astype(F32), ((0, 8 - TOPK), (0, 0)), constant_values=-1.0)
-    probs = jnp.pad(gate_probs.T, ((0, 8 - TOPK), (0, 0)))
-    meta = jnp.tile(jnp.concatenate([ids, probs], axis=0), (1, 2))
     vmem = pl.BlockSpec(memory_space=pltpu.VMEM)
     anywhere = pl.BlockSpec(memory_space=pl.ANY)
     v = pltpu.VMEM
@@ -435,32 +469,36 @@
         v((D, 2 * FF), BF), v((D, FF), BF),
         v((ROWS, 2 * FF), F32), v((ROWS, FF), BF), v((ROWS, 2 * FF), BF),
         v((ROWS, D), BF), v((ROWS, D), BF),
-        v((4, GR, GR), BF), v((4, GR, GR), F32),
+        v((16, GR), F32), v((4, GR, GR), BF), v((4, GR, GR), F32),
         v((2, 4, TOK, D), BF), v((2, 4, TOK, D), BF), v((2, 4, TOK, D), BF), v((2, 4, TOK, D), BF),
         v((2, 4, 8, GR), F32), v((2, 4, 8, GR), F32), v((TOK, D), F32), v((TOK, D), F32),
-        *block, v((DY, FF), F32), *wide, v((DY, 2 * FF), F32),
-        pltpu.SemaphoreType.DMA((192,)), pltpu.SemaphoreType.DMA((192,)), pltpu.SemaphoreType.DMA((8,)),
+        *block, *wide,
+        pltpu.SemaphoreType.DMA((208,)), pltpu.SemaphoreType.DMA((208,)), pltpu.SemaphoreType.DMA((8,)),
     ]
-    grad = jax.ShapeDtypeStruct((DY, FF), F32)
-    mixed, token_grads, prob_grads, grad_gate, grad_up, grad_down = pl.pallas_call(
+    shapes = [((TOK, D), BF), ((TOK, D), BF), ((8, GR), F32)] + [((DY, FF), F32)] * 3
+    held = pl.pallas_call(
         kernel,
-        out_shape=(
-            jax.ShapeDtypeStruct((TOK, D), BF),
-            jax.ShapeDtypeStruct((TOK, D), BF),
-            jax.ShapeDtypeStruct((8, GR), F32),
-            grad, grad, grad,
-        ),
-        in_specs=[vmem] * 3 + [anywhere] * 3,
-        out_specs=(vmem,) * 3 + (anywhere,) * 3,
+        out_shape=tuple(pltpu.VMEM(shape, dtype) for shape, dtype in shapes),
+        in_specs=[vmem] * 4 + [anywhere] * 3,
+        out_specs=(vmem,) * 6,
         scratch_shapes=scratch,
         name="expert_layer",
         compiler_params=pltpu.CompilerParams(
-            collective_id=0, has_side_effects=True, vmem_limit_bytes=67043328
+            collective_id=0, has_side_effects=True, vmem_limit_bytes=VMEM_LIMIT
         ),
-    )(tokens, cotangent, meta, gate_proj[0], up_proj[0], down_proj[0])
+    )(tokens, cotangent, expert_ids.T, gate_probs.T, gate_proj[0], up_proj[0], down_proj[0])
+    shapes[2] = ((TOPK, TOK), F32)
+    mixed, token_grads, prob_grads, grad_gate, grad_up, grad_down = pl.pallas_call(
+        write_out,
+        out_shape=tuple(jax.ShapeDtypeStruct(shape, dtype) for shape, dtype in shapes),
+        in_specs=[vmem] * 6,
+        out_specs=(anywhere, anywhere, vmem, anywhere, anywhere, anywhere),
+        scratch_shapes=[pltpu.SemaphoreType.DMA((5,))],
+        name="write_out",
+        compiler_params=pltpu.CompilerParams(vmem_limit_bytes=1024 * 1024),
+    )(*(pltpu.with_memory_space_constraint(part, pltpu.VMEM) for part in held))
     return (
-        mixed, token_grads, prob_grads[:TOPK, :TOK].T,
-        grad_gate[None], grad_up[None], grad_down[None],
+        mixed, token_grads, prob_grads.T, grad_gate[None], grad_up[None], grad_down[None],
     )
 
 

time: 183 us -> 171 us (0.934)
  local copies, waits for them, and re-layouts: 11.2 us -> 0 us
    unnamed x9 -> x0, local copies, waits for them, and re-layouts: 9.23 us -> none
    pallas_call x1 -> x2, Pallas kernels: 169 us -> 169 us  [the longest x1 166 us: layer(): pl.pallas_call(kernel, out_shape=tuple((pltpu.VMEM(shape, dtype) for shap...]
where the time goes in v3:
time: 171 us; the launch traced here: 170 us
  Pallas kernels  169 us (99%)
    pallas_call x1, Pallas kernels, layer(): pl.pallas_call(kernel, out_shape=tuple((pltpu.VMEM(shape, dtype) for shap...  166 us

profile of v3, /device:TPU:2, one launch (start us, length us, event | category | flops | bytes accessed | tf_op | source)
XLA Modules:
  0.0 170.3 jit_solution(12792808528990850968)
XLA Ops:
  0.6 166.5 %expert_layer.1 = (bf16[64,2048]{1,0:T(8,128)(2,1)S(1)}, bf16[64,2048]{1,0:T(8,128)(2,1)S(1)}, f32[8,128]{1,0:T(8,128)S(1)}, f32[512,768]{1,0:T(8,128)S(1)}, f32...) custom-call(bf16[64,2048]{1,0:T(8,128)(2,1)} %tok.1, bf16[64,2048]{1,0:T(8,128)(2,1)} %cot.1, s32[6,64]{1,0:T(8,128)} %bitcast.12, ...), custom_call_target="tpu_custom_call" | custom-call | tf_op jit(solution)/shard_map/expert_layer/pallas_call | solution.py:479
  167.1 3.0 %write_out.1 = (bf16[64,2048]{1,0:T(8,128)(2,1)}, bf16[64,2048]{1,0:T(8,128)(2,1)}, f32[6,64]{1,0:T(8,128)}, f32[512,768]{1,0:T(8,128)}, f32[512,768]{1,0:T(8,128)}, /*index=5*/f32[512,768]{1,0:T(8,128)}) custom-call(bf16[64,2048]{1,0:T(8,128)(2,1)S(1)} %get-tuple-element.18.mixed, bf16[64,2048]{1,0:T(8,128)(2,1)S(1)} %get-tuple-element.19.tgrad, ...), custom_call_target="tpu_custom_call" | custom-call | tf_op jit(solution)/shard_map/write_out/pallas_call | solution.py:491

commit v4 on v3

--- a/solution.py
+++ b/solution.py
@@ -30,7 +30,7 @@
     meta, pm, wm, zs_o, zr_o, zs_d, zr_d, pgs, pgr, acc_o, acc_d,
     d1, d2, d3, dhp, dhm, dfp, dfm,
     g1, g2, g3, ghp, ghm, gfp, gfm,
-    ssem, rsem, lsem,
+    ids_v, probs_v, go, ssem, rsem, lsem,
 ):
     y = lax.axis_index("dp")
     e = lax.axis_index("expert")
@@ -48,10 +48,27 @@
     from_x = [at(dx=-dx, dc=dc) for dx, dc in offsets]
 
     barrier = pltpu.get_barrier_semaphore()
-    peers = [yp, ym, zp, zq] + to_x[1:]
-    for peer in peers:
+
+    def tell(peer):
         pl.semaphore_signal(barrier, inc=1, device_id=peer, device_id_type=MESH)
-    pl.semaphore_wait(barrier, len(peers))
+
+    other, first, second = at(dc=1), (NC - c) % NC, 1 - c
+    for dy in (1, -1):
+        tell(at(dy=dy, dc=first))
+    for dz in (1, -1):
+        tell(at(dz=dz, dc=second))
+    for dx in range(1, NX):
+        tell(at(dx=dx, dc=second))
+    tell(other)
+
+    @pl.when(c == 0)
+    def _():
+        pl.semaphore_wait(barrier, NC * 2 + 1)
+        pl.semaphore_signal(go, inc=1, device_id=other, device_id_type=MESH)
+
+    @pl.when(c == 1)
+    def _():
+        pl.semaphore_wait(go, 1)
 
     used = [0, 0]
     started = []
@@ -100,6 +117,7 @@
 
     gate_own = own(gw, gu, gcol)
     up_own = own(uw, gu, ucol)
+    tables = [local(ids, ids_v), local(probs, probs_v)]
 
     def zblock(buf, j, zi, start=0, size=TOK):
         return buf.at[pl.ds(j * GR + zi * TOK + start, size), :]
@@ -125,10 +143,22 @@
             return send(zm.at[s - 1, 0], zm.at[s, 0], zp), send(zm.at[s - 1, 1], zm.at[s, 1], zq)
         return (send(zm.at[2, 0], zm.at[3, 1], zp),)
 
+    for copy in tables:
+        copy.wait()
     meta[...] = jnp.full(meta.shape, -1.0, F32)
     for start in (0, TOK):
-        meta[0:TOPK, start : start + TOK] = ids[...].astype(F32)
-        meta[8 : 8 + TOPK, start : start + TOK] = probs[...]
+        meta[0:TOPK, start : start + TOK] = ids_v[...].astype(F32)
+        meta[8 : 8 + TOPK, start : start + TOK] = probs_v[...]
+
+    @pl.when(c == 1)
+    def _():
+        pl.semaphore_wait(barrier, 1 + NC * 2 + NC * (NX - 1))
+        pl.semaphore_signal(go, inc=1, device_id=other, device_id_type=MESH)
+
+    @pl.when(c == 0)
+    def _():
+        pl.semaphore_wait(go, 1)
+
     m_now = mstep(0)
     t_now = zstep(zt, tok, 0)
     loads = [
@@ -215,7 +245,7 @@
             copy.wait_recv()
         if s < 4:
             c_now = zstep(zc, cot, s)
-        if s == 3:
+        if s == 1:
             up_far = relay(up_own, gu, ucol)
             down_own = own(dw, dn, slice(None))
         dispatch_grads(s - 1)
@@ -473,6 +503,7 @@
         v((2, 4, TOK, D), BF), v((2, 4, TOK, D), BF), v((2, 4, TOK, D), BF), v((2, 4, TOK, D), BF),
         v((2, 4, 8, GR), F32), v((2, 4, 8, GR), F32), v((TOK, D), F32), v((TOK, D), F32),
         *block, *wide,
+        v((TOPK, TOK), jnp.int32), v((TOPK, TOK), F32), pltpu.SemaphoreType.REGULAR,
         pltpu.SemaphoreType.DMA((208,)), pltpu.SemaphoreType.DMA((208,)), pltpu.SemaphoreType.DMA((8,)),
     ]
     shapes = [((TOK, D), BF), ((TOK, D), BF), ((8, GR), F32)] + [((DY, FF), F32)] * 3

time: 171 us -> 168 us (0.982)
  Pallas kernels: 169 us -> 165 us
    pallas_call x1, Pallas kernels: 166 us -> 162 us  [layer(): pl.pallas_call(kernel, out_shape=tuple((pltpu.VMEM(shape, dtype) for shap...]
where the time goes in v4:
time: 168 us; the launch traced here: 166 us
  Pallas kernels  165 us (98%)
    pallas_call x1, Pallas kernels, layer(): pl.pallas_call(kernel, out_shape=tuple((pltpu.VMEM(shape, dtype) for shap...  162 us

profile of v4, /device:TPU:2, one launch (start us, length us, event | category | flops | bytes accessed | tf_op | source)
XLA Modules:
  0.0 165.9 jit_solution(12616171442566449588)
XLA Ops:
  0.6 162.1 %expert_layer.1 = (bf16[64,2048]{1,0:T(8,128)(2,1)S(1)}, bf16[64,2048]{1,0:T(8,128)(2,1)S(1)}, f32[8,128]{1,0:T(8,128)S(1)}, f32[512,768]{1,0:T(8,128)S(1)}, f32...) custom-call(bf16[64,2048]{1,0:T(8,128)(2,1)} %tok.1, bf16[64,2048]{1,0:T(8,128)(2,1)} %cot.1, s32[6,64]{1,0:T(8,128)} %bitcast.12, ...), custom_call_target="tpu_custom_call" | custom-call | tf_op jit(solution)/shard_map/expert_layer/pallas_call | solution.py:510
  162.7 3.0 %write_out.1 = (bf16[64,2048]{1,0:T(8,128)(2,1)}, bf16[64,2048]{1,0:T(8,128)(2,1)}, f32[6,64]{1,0:T(8,128)}, f32[512,768]{1,0:T(8,128)}, f32[512,768]{1,0:T(8,128)}, /*index=5*/f32[512,768]{1,0:T(8,128)}) custom-call(bf16[64,2048]{1,0:T(8,128)(2,1)S(1)} %get-tuple-element.18.mixed, bf16[64,2048]{1,0:T(8,128)(2,1)S(1)} %get-tuple-element.19.tgrad, ...), custom_call_target="tpu_custom_call" | custom-call | tf_op jit(solution)/shard_map/write_out/pallas_call | solution.py:522

commit v5 on v4

--- a/solution.py
+++ b/solution.py
@@ -510,7 +510,7 @@
     held = pl.pallas_call(
         kernel,
         out_shape=tuple(pltpu.VMEM(shape, dtype) for shape, dtype in shapes),
-        in_specs=[vmem] * 4 + [anywhere] * 3,
+        in_specs=[anywhere] * 7,
         out_specs=(vmem,) * 6,
         scratch_shapes=scratch,
         name="expert_layer",

time: 168 us -> 167 us (level)
  no operation moved by 1% of the time
where the time goes in v5:
time: 167 us; the launch traced here: 165 us
  Pallas kernels  164 us (98%)
    pallas_call x1, Pallas kernels, layer(): pl.pallas_call(kernel, out_shape=tuple((pltpu.VMEM(shape, dtype) for shap...  161 us

profile of v5, /device:TPU:2, one launch (start us, length us, event | category | flops | bytes accessed | tf_op | source)
XLA Modules:
  0.0 164.9 jit_solution(17654414201893852201)
XLA Ops:
  0.6 161.1 %expert_layer.1 = (bf16[64,2048]{1,0:T(8,128)(2,1)S(1)}, bf16[64,2048]{1,0:T(8,128)(2,1)S(1)}, f32[8,128]{1,0:T(8,128)S(1)}, f32[512,768]{1,0:T(8,128)S(1)}, f32...) custom-call(bf16[64,2048]{1,0:T(8,128)(2,1)} %tok.1, bf16[64,2048]{1,0:T(8,128)(2,1)} %cot.1, s32[6,64]{1,0:T(8,128)} %bitcast.12, ...), custom_call_target="tpu_custom_call" | custom-call | tf_op jit(solution)/shard_map/expert_layer/pallas_call | solution.py:510
  161.8 3.0 %write_out.1 = (bf16[64,2048]{1,0:T(8,128)(2,1)}, bf16[64,2048]{1,0:T(8,128)(2,1)}, f32[6,64]{1,0:T(8,128)}, f32[512,768]{1,0:T(8,128)}, f32[512,768]{1,0:T(8,128)}, /*index=5*/f32[512,768]{1,0:T(8,128)}) custom-call(bf16[64,2048]{1,0:T(8,128)(2,1)S(1)} %get-tuple-element.18.mixed, bf16[64,2048]{1,0:T(8,128)(2,1)S(1)} %get-tuple-element.19.tgrad, ...), custom_call_target="tpu_custom_call" | custom-call | tf_op jit(solution)/shard_map/write_out/pallas_call | solution.py:522

commit v6 on v5

--- a/solution.py
+++ b/solution.py
@@ -231,7 +231,7 @@
             copy.wait_recv()
         if s < 4:
             t_now = zstep(zt, tok, s)
-        if s == 3:
+        if s == 2:
             gate_far = relay(gate_own, gu, gcol)
         if s == 3:
             c_now = zstep(zc, cot, 0)

time: 167 us -> 167 us (level)
  no operation moved by 1% of the time
where the time goes in v6:
time: 167 us; the launch traced here: 165 us
  Pallas kernels  164 us (98%)
    pallas_call x1, Pallas kernels, layer(): pl.pallas_call(kernel, out_shape=tuple((pltpu.VMEM(shape, dtype) for shap...  161 us

profile of v6, /device:TPU:2, one launch (start us, length us, event | category | flops | bytes accessed | tf_op | source)
XLA Modules:
  0.0 164.9 jit_solution(18090990006310925193)
XLA Ops:
  0.6 161.1 %expert_layer.1 = (bf16[64,2048]{1,0:T(8,128)(2,1)S(1)}, bf16[64,2048]{1,0:T(8,128)(2,1)S(1)}, f32[8,128]{1,0:T(8,128)S(1)}, f32[512,768]{1,0:T(8,128)S(1)}, f32...) custom-call(bf16[64,2048]{1,0:T(8,128)(2,1)} %tok.1, bf16[64,2048]{1,0:T(8,128)(2,1)} %cot.1, s32[6,64]{1,0:T(8,128)} %bitcast.12, ...), custom_call_target="tpu_custom_call" | custom-call | tf_op jit(solution)/shard_map/expert_layer/pallas_call | solution.py:510
  161.8 3.0 %write_out.1 = (bf16[64,2048]{1,0:T(8,128)(2,1)}, bf16[64,2048]{1,0:T(8,128)(2,1)}, f32[6,64]{1,0:T(8,128)}, f32[512,768]{1,0:T(8,128)}, f32[512,768]{1,0:T(8,128)}, /*index=5*/f32[512,768]{1,0:T(8,128)}) custom-call(bf16[64,2048]{1,0:T(8,128)(2,1)S(1)} %get-tuple-element.18.mixed, bf16[64,2048]{1,0:T(8,128)(2,1)S(1)} %get-tuple-element.19.tgrad, ...), custom_call_target="tpu_custom_call" | custom-call | tf_op jit(solution)/shard_map/write_out/pallas_call | solution.py:522
